TPU v7x, 512 devices: a whole 4x8x8 slice. The times are simulated.
512 devices in a mesh: wide: 64 (over z, y), narrow: 8 (over x, core).
Axes of the slice: x: 4, y: 8, z: 8, core: 2. Of those that a mesh axis runs over, the one named last changes fastest.
Arguments:
- pixel_slabs: bfloat16 [256, 3, 64, 128], P('wide', None, 'narrow'), may hold values from -1 to 1
- conv_in_weight: bfloat16 [3, 3, 96, 9], replicated, may hold values from -0.625 to 0.625
- conv_in_bias: float32 [96], replicated, may hold values from -3 to 3
- norm_gain: float32 [96], replicated, may hold values from 0.5 to 1.5
- conv_weight: bfloat16 [3, 3, 96, 288], replicated, may hold values from -0.125 to 0.125
- conv_bias: float32 [96], replicated, may hold values from -3 to 3
- clip_lengths: int32 [6], replicated, may hold values from 1 to 81, 256 in all
- slab_place: int32 [256], replicated, may hold values from 0 to 255, as said below
- tok_place: int32 [65536], replicated, may hold values from 0 to 65535, as said below
Outputs:
- seq_features: bfloat16 [524288, 384], P(('wide', 'narrow'))
Inputs may be any that keep to these rules, and one draw needn't show every extreme that they name: `slab_place`: A permutation. The 4 entries of one aligned block (slabs of one index of wide) name exactly 4 distinct owners (value // 4), each exactly once. `tok_place`: A permutation. The 1024 entries of one aligned block (patch rows of one index of wide) name exactly 32 distinct sequence blocks (value // 1024), exactly 32 entries each.
All inputs are finite; a program needn't handle non-finite values.
Results may differ from a plain program's by a relative error of at most 0.0065.
Values may be sent and summed in bfloat16 or wider, within the bound.
A program may use at most 64 MiB of HBM per device.

v0:
```python
import jax
import jax.numpy as jnp
from jax import lax
from jax.sharding import PartitionSpec as P

EPSILON = 1e-06


def with_halo(block, sides, width):
    for axis, dim in sides:
        count = lax.axis_size(axis)
        forward = [(i, i + 1) for i in range(count - 1)]
        backward = [(target, source) for source, target in forward]
        low = lax.ppermute(
            lax.slice_in_dim(block, block.shape[dim] - width, None, axis=dim), axis, forward
        )
        high = lax.ppermute(lax.slice_in_dim(block, 0, width, axis=dim), axis, backward)
        block = jnp.concatenate([low, block, high], axis=dim)
    return block


def from_behind(array, axis, by):
    count = lax.axis_size(axis)
    pairs = [(i, i + by) for i in range(count) if 0 <= i + by < count]
    return lax.ppermute(array, axis, pairs)


def tap_valid(clip_lengths, frame_ids):
    starts = jnp.cumsum(clip_lengths) - clip_lengths
    reached = starts[None, :] <= frame_ids[:, None]
    latest = jnp.max(jnp.where(reached, starts[None, :], -1), axis=1)
    offsets = jnp.where(frame_ids >= 0, frame_ids - latest, -1)
    reach_back = jnp.array([2, 1, 0], jnp.int32)
    return offsets[:, None] >= reach_back[None, :]


def causal_conv(padded_in, valid_taps, weight, bias_vec):
    frame_count = valid_taps.shape[0]
    row_count = padded_in.shape[2] - 2
    col_count = padded_in.shape[3]
    tap_list = []
    for time_tap in range(3):
        keep = valid_taps[:, time_tap].astype(padded_in.dtype)
        tap_list.append(padded_in[time_tap : time_tap + frame_count] * keep[:, None, None, None])
    stacked = jnp.concatenate(tap_list, axis=1)
    stacked = jnp.pad(stacked, ((0, 0), (0, 0), (0, 0), (1, 1)))
    running = jnp.zeros((frame_count, weight.shape[2], row_count, col_count), jnp.float32)
    for row_tap in range(3):
        for col_tap in range(3):
            window = stacked[:, :, row_tap : row_tap + row_count, col_tap : col_tap + col_count]
            running = running + jnp.einsum(
                "ok,fkyx->foyx",
                weight[row_tap, col_tap],
                window,
                preferred_element_type=jnp.float32,
            )
    return running + bias_vec[None, :, None, None]


def norm_silu(hidden, norm_gain):
    values = hidden.astype(jnp.float32)
    mean_square = jnp.mean(values * values, axis=1, keepdims=True)
    scaled = values * lax.rsqrt(mean_square + EPSILON) * norm_gain[None, :, None, None]
    return jax.nn.silu(scaled).astype(jnp.bfloat16)


def borders(frames_in, width, depth):
    haloed = with_halo(frames_in, (("narrow", 2),), width)
    earlier = from_behind(haloed[-depth:], "wide", 1)
    return jnp.concatenate([earlier, haloed], axis=0)


def route_plan(places, source, per_device, capacity):
    owners = places // per_device
    counter = jnp.arange(per_device, dtype=jnp.int32)
    own_owners = lax.dynamic_slice_in_dim(owners, source * per_device, per_device, 0)
    sorted_at = jnp.argsort(own_owners, stable=True)
    sorted_send = own_owners[sorted_at] * capacity + counter % capacity
    send_index = sorted_send[jnp.argsort(sorted_at)]
    outside = (owners != source).astype(jnp.int32)
    arrivals = jnp.argsort(outside, stable=True)[:per_device]
    buffer_pos = arrivals // per_device * capacity + counter % capacity
    arrival_slots = places[arrivals] % per_device
    gather_index = buffer_pos[jnp.argsort(arrival_slots)]
    return (send_index, gather_index)


def patch_rows(summed):
    frame_count, channels, row_count, col_count = summed.shape
    blocks = summed.reshape(frame_count, channels, row_count // 2, 2, col_count // 2, 2)
    reordered = jnp.transpose(blocks, (0, 2, 4, 3, 5, 1))
    return reordered.reshape(-1, 4 * channels).astype(jnp.bfloat16)


def body(
    pixel_slabs,
    conv_in_weight,
    conv_in_bias,
    norm_gain,
    conv_weight,
    conv_bias,
    clip_lengths,
    slab_place,
    tok_place,
):
    wide_count = lax.axis_size("wide")
    wide_index = lax.axis_index("wide")
    frame_count = pixel_slabs.shape[0]
    slab_cap = frame_count // min(wide_count // 2, frame_count)
    send_index, gather_index = route_plan(slab_place, wide_index, frame_count, slab_cap)
    outgoing = (
        jnp.zeros((wide_count * slab_cap,) + pixel_slabs.shape[1:], pixel_slabs.dtype)
        .at[send_index]
        .set(pixel_slabs)
    )
    arrived = lax.all_to_all(outgoing, "wide", split_axis=0, concat_axis=0, tiled=True)
    frames_in = arrived[gather_index]
    first_frame = wide_index * frame_count
    own_frames = first_frame + jnp.arange(frame_count, dtype=jnp.int32)
    valid_taps = tap_valid(clip_lengths, own_frames)
    pixel_full = borders(frames_in, 1, 2)
    hidden = causal_conv(pixel_full, valid_taps, conv_in_weight, conv_in_bias).astype(jnp.bfloat16)
    active_full = borders(norm_silu(hidden, norm_gain), 1, 2)
    branch = causal_conv(active_full, valid_taps, conv_weight, conv_bias)
    tokens = patch_rows(hidden.astype(jnp.float32) + branch)
    tok_count = tokens.shape[0]
    tok_cap = tok_count // min(wide_count // 2, tok_count)
    send_tok, gather_tok = route_plan(tok_place, wide_index, tok_count, tok_cap)
    parcel = (
        jnp.zeros((wide_count * tok_cap, tokens.shape[1]), tokens.dtype).at[send_tok].set(tokens)
    )
    delivered = lax.all_to_all(parcel, "wide", split_axis=0, concat_axis=0, tiled=True)
    return delivered[gather_tok]


def solution(mesh):
    placed = (P("wide", None, "narrow", None), P(), P(), P(), P(), P(), P(), P(), P())
    return jax.shard_map(
        body, mesh=mesh, in_specs=placed, out_specs=P(("wide", "narrow"), None), check_vma=False
    )
```

profile of v0, /device:TPU:1, one launch (start us, length us, event | category | flops | bytes accessed | tf_op | source)
XLA Modules:
  0.0 181.5 jit_solution(16640564884330059926)
XLA Ops:
  4.4 2.0 %scatter_fusion = bf16[64,3,8,128]{3,2,1,0:T(8,128)(2,1)} fusion(bf16[64,3,8,128]{3,2,1,0:T(8,128)(2,1)} %broadcast_in_dim.35, s32[4]{0:T(128)S(1)} %fusion.73, bf16[4,3,8,128]{3,2,1,0:T(8,128)(2,1)} %param.10), kind=kCustom, calls=%fused_computation.10 | custom fusion | bytes 73744 | tf_op jit(solution)/shard_map/scatter | solution.py:114
  6.4 17.1 %all-to-all-start = ((bf16[64,3,8,128]{3,2,1,0:T(8,128)(2,1)}), bf16[64,3,8,128]{3,2,1,0:T(8,128)(2,1)S(1)}, u32[]{:S(2)}, u32[]{:S(2)}) async-start(bf16[64,3,8,128]{3,2,1,0:T(8,128)(2,1)} %scatter_fusion), calls=%async_computation | async-start | bytes 786432 | tf_op jit(solution)/shard_map/all_to_all | solution.py:116
  23.7 3.2 %sort.134 = (s32[256]{0:T(256)}, s32[256]{0:T(256)S(1)}) sort(s32[256]{0:T(256)S(1)} %get-tuple-element.21, s32[256]{0:T(256)S(1)} %iota.48), dimensions={0}, to_apply=%region_5.6 | sort | flops 2048 | bytes 4096 | tf_op jit(solution)/shard_map/jit(argsort)/sort | solution.py:81
  28.6 4.4 %sort.130 = (s32[1024]{0:T(1024)}, s32[1024]{0:T(1024)S(1)}) sort(s32[1024]{0:T(1024)S(1)} %dynamic_slice.6, s32[1024]{0:T(1024)S(1)} %iota.43), dimensions={0}, to_apply=%region_0.1 | sort | flops 10240 | bytes 16384 | tf_op jit(solution)/shard_map/jit(argsort)/sort | solution.py:77
  33.0 4.4 %sort.131 = (s32[1024]{0:T(1024)}, s32[1024]{0:T(1024)S(1)}) sort(s32[1024]{0:T(1024)S(1)} %get-tuple-element.13, s32[1024]{0:T(1024)S(1)} %iota.45), dimensions={0}, to_apply=%region_1.2 | sort | flops 10240 | bytes 16384 | tf_op jit(solution)/shard_map/jit(argsort)/sort | solution.py:79
  39.2 6.3 %collective-permute-start = (bf16[4,3,1,128]{3,1,2,0:T(4,128)(2,1)S(1)}, bf16[4,3,1,128]{3,1,2,0:T(4,128)(2,1)S(1)}, u32[]{:S(2)}, u32[]{:S(2)}) collective-permute-start(bf16[4,3,1,128]{3,1,2,0:T(4,128)(2,1)S(1)} %copy.94), channel_id=1, source_target_pairs={{0,1},{1,2},{2,3},{3,4},{4,5},{5,6},{6,7},{8,9},{9,10},{10,11},{11... | collective-permute-start | bytes 9224 | tf_op jit(solution)/shard_map/ppermute | solution.py:14
  45.5 1.9 %collective-permute-start.1 = (bf16[4,3,1,128]{3,1,2,0:T(4,128)(2,1)S(1)}, bf16[4,3,1,128]{3,1,2,0:T(4,128)(2,1)S(1)}, u32[]{:S(2)}, u32[]{:S(2)}) collective-permute-start(bf16[4,3,1,128]{3,1,2,0:T(4,128)(2,1)S(1)} %copy.95), channel_id=1, source_target_pairs={{1,0},{2,1},{3,2},{4,3},{5,4},{6,5},{7,6},{9,8},{10,9},{11,10},{12... | collective-permute-start | bytes 9224 | tf_op jit(solution)/shard_map/ppermute | solution.py:17
  47.5 2.9 %collective-permute-done.1 = bf16[4,3,1,128]{3,1,2,0:T(4,128)(2,1)S(1)} collective-permute-done((bf16[4,3,1,128]{3,1,2,0:T(4,128)(2,1)S(1)}, bf16[4,3,1,128]{3,1,2,0:T(4,128)(2,1)S(1)}, u32[]{:S(2)}, u32[]{:S(2)}) %collective-permute-start.1) | collective-permute-done | bytes 3104 | tf_op jit(solution)/shard_map/ppermute | solution.py:17
  50.5 2.8 %collective-permute-start.2 = (bf16[2,3,10,128]{3,1,2,0:T(4,128)(2,1)S(1)}, bf16[2,3,10,128]{3,1,2,0:T(4,128)(2,1)S(1)}, u32[]{:S(2)}, u32[]{:S(2)}) collective-permute-start(bf16[2,3,10,128]{3,1,2,0:T(4,128)(2,1)S(1)} %slice.235), channel_id=1, source_target_pairs={{0,8},{8,16},{16,24},{24,32},{32,40},{40,48},{48,56},{56,64},{64,7... | collective-permute-start | bytes 46088 | tf_op jit(solution)/shard_map/ppermute | solution.py:25
  57.8 1.1 fusion.12
  59.5 2.8 %collective-permute-start.3 = (bf16[4,96,1,128]{3,1,2,0:T(8,128)(2,1)S(1)}, bf16[4,96,1,128]{3,1,2,0:T(8,128)(2,1)S(1)}, u32[]{:S(2)}, u32[]{:S(2)}) collective-permute-start(bf16[4,96,1,128]{3,1,2,0:T(8,128)(2,1)S(1)} %get-tuple-element.27), channel_id=1, source_target_pairs={{0,1},{1,2},{2,3},{3,4},{4,5},{5,6},{6,7},{8,9},{9,10},{10,11},{11... | collective-permute-start | bytes 294920 | tf_op jit(solution)/shard_map/ppermute | solution.py:14
  62.3 2.1 %collective-permute-start.4 = (bf16[4,96,1,128]{3,1,2,0:T(8,128)(2,1)S(1)}, bf16[4,96,1,128]{3,1,2,0:T(8,128)(2,1)S(1)}, u32[]{:S(2)}, u32[]{:S(2)}) collective-permute-start(bf16[4,96,1,128]{3,1,2,0:T(8,128)(2,1)S(1)} %get-tuple-element.28), channel_id=1, source_target_pairs={{1,0},{2,1},{3,2},{4,3},{5,4},{6,5},{7,6},{9,8},{10,9},{11,10},{12... | collective-permute-start | bytes 294920 | tf_op jit(solution)/shard_map/ppermute | solution.py:17
  64.6 25.3 %sort.136 = (s32[65536]{0:T(1024)}, s32[65536]{0:T(1024)}) sort(s32[65536]{0:T(1024)S(1)} %compare_convert_fusion, s32[65536]{0:T(1024)S(1)} %iota.51), dimensions={0}, to_apply=%region_11.12 | sort | flops 1048576 | bytes 1048576 | tf_op jit(solution)/shard_map/jit(argsort)/sort | solution.py:81
  90.9 3.9 %collective-permute-start.5 = (bf16[2,96,10,128]{3,1,2,0:T(8,128)(2,1)}, bf16[2,96,10,128]{3,1,2,0:T(8,128)(2,1)S(1)}, u32[]{:S(2)}, u32[]{:S(2)}) collective-permute-start(bf16[2,96,10,128]{3,1,2,0:T(8,128)(2,1)} %slice.240), channel_id=1, source_target_pairs={{0,8},{8,16},{16,24},{24,32},{32,40},{40,48},{48,56},{56,64},{64,7... | collective-permute-start | bytes 1474568 | tf_op jit(solution)/shard_map/ppermute | solution.py:25
  95.5 4.7 %gather_fusion = s32[1024]{0:T(1024)S(1)} fusion(s32[1024]{0:T(1024)S(1)} %dynamic_slice.6, s32[1024]{0:T(1024)S(1)} %get-tuple-element.52), kind=kCustom, calls=%fused_computation | custom fusion | bytes 12288 | tf_op jit(solution)/shard_map/gather | solution.py:78
  100.3 4.5 %gather_fusion.1 = s32[1024]{0:T(1024)S(1)} fusion(s32[1024]{0:T(1024)S(1)} %fusion.66, s32[1024]{0:T(1024)S(1)} %get-tuple-element.53), kind=kCustom, calls=%fused_computation.1 | custom fusion | bytes 12288 | tf_op jit(solution)/shard_map/gather | solution.py:79
  113.5 1.6 fusion.22
  117.2 6.4 %scatter_custom_fusion.1 = bf16[2048,384]{1,0:T(8,128)(2,1)} fusion(s32[1024]{0:T(1024)S(1)} %bitcast.179, bf16[1024,384]{1,0:T(8,128)(2,1)S(1)} %reshape.226, bf16[]{:T(256)} %constant.120.clone.1), kind=kCustom, calls=%fused_computation.50 | custom fusion | bytes 1572866 | tf_op jit(solution)/shard_map/scatter | solution.py:130
  123.6 13.2 %all-to-all-start.1 = ((bf16[64,32,384]{2,1,0:T(8,128)(2,1)}), bf16[64,32,384]{2,1,0:T(8,128)(2,1)S(1)}, u32[]{:S(2)}, u32[]{:S(2)}) async-start(bf16[64,32,384]{2,1,0:T(8,128)(2,1)} %bitcast.69), calls=%async_computation.1 | async-start | bytes 3145728 | tf_op jit(solution)/shard_map/all_to_all | solution.py:132
  136.8 6.2 %gather_fusion.7 = s32[1024]{0:T(1024)S(1)} fusion(s32[65536]{0:T(1024)S(1)} %copy-done.1, s32[1024]{0:T(1024)S(1)} %get-tuple-element.29), kind=kCustom, calls=%fused_computation.7 | custom fusion | bytes 12288 | tf_op jit(solution)/shard_map/gather | solution.py:83
  142.9 4.4 %sort.137 = (s32[1024]{0:T(1024)}, s32[1024]{0:T(1024)S(1)}) sort(s32[1024]{0:T(1024)S(1)} %add_select_fusion.1, s32[1024]{0:T(1024)S(1)} %iota.52), dimensions={0}, to_apply=%region_12.13 | sort | flops 10240 | bytes 16384 | tf_op jit(solution)/shard_map/jit(argsort)/sort | solution.py:84
  147.3 4.5 %gather_fusion.8 = s32[1024]{0:T(1024)S(1)} fusion(s32[1024]{0:T(1024)S(1)} %get-tuple-element.30, s32[1024]{0:T(1024)S(1)} %fusion.61), kind=kCustom, calls=%fused_computation.8 | custom fusion | bytes 12288 | tf_op jit(solution)/shard_map/gather | solution.py:84
  151.9 24.6 %all-to-all-done.1 = bf16[64,32,384]{2,1,0:T(8,128)(2,1)S(1)} async-done(((bf16[64,32,384]{2,1,0:T(8,128)(2,1)}), bf16[64,32,384]{2,1,0:T(8,128)(2,1)S(1)}, u32[]{:S(2)}, u32[]{:S(2)}) %all-to-all-start.1) | async-done | bytes 1572896 | tf_op jit(solution)/shard_map/all_to_all | solution.py:132
  176.5 5.0 %gather_fusion.9 = bf16[1024,384]{1,0:T(8,128)(2,1)} fusion(bf16[2048,384]{1,0:T(8,128)(2,1)S(1)} %bitcast.174, s32[1024]{0:T(1024)S(1)} %broadcast_clamp_fusion), kind=kCustom, calls=%fused_computation.9 | custom fusion | bytes 1576960 | tf_op jit(solution)/shard_map/gather | solution.py:133
  (108 shorter events, 25.8 us)
Async XLA Ops:
  0.0 27.0 %copy-start = (s32[256]{0:T(256)S(1)}, s32[256]{0:T(256)}, u32[]{:S(2)}) copy-start(s32[256]{0:T(256)} %param.17) | copy-start | bytes 3076
  0.0 23.6 %copy-start.7 = (s32[6]{0:T(128)S(1)}, s32[6]{0:T(128)}, u32[]{:S(2)}) copy-start(s32[6]{0:T(128)} %param.16) | copy-start | bytes 76
  0.0 28.5 %copy-start.1 = (s32[65536]{0:T(1024)S(1)}, s32[65536]{0:T(1024)}, u32[]{:S(2)}) copy-start(s32[65536]{0:T(1024)} %param.18) | copy-start | bytes 786436
  3.6 34.6 %copy-start.3 = (bf16[3,3,96,9]{2,1,3,0:T(4,128)(2,1)S(1)}, bf16[3,3,96,9]{2,1,3,0:T(4,128)(2,1)}, u32[]{:S(2)}) copy-start(bf16[3,3,96,9]{2,1,3,0:T(4,128)(2,1)} %param.11) | copy-start | bytes 46660
  3.6 41.8 %copy-start.8 = (s32[3]{0:T(128)S(1)}, s32[3]{0:T(128)}, u32[]{:S(2)}) copy-start(s32[3]{0:T(128)} %constant.143.clone) | copy-start | bytes 40
  6.4 32.2 %all-to-all-start = ((bf16[64,3,8,128]{3,2,1,0:T(8,128)(2,1)}), bf16[64,3,8,128]{3,2,1,0:T(8,128)(2,1)S(1)}, u32[]{:S(2)}, u32[]{:S(2)}) async-start(bf16[64,3,8,128]{3,2,1,0:T(8,128)(2,1)} %scatter_fusion), calls=%async_computation | async-start | bytes 786432 | tf_op jit(solution)/shard_map/all_to_all | solution.py:116
  39.2 8.3 %collective-permute-start = (bf16[4,3,1,128]{3,1,2,0:T(4,128)(2,1)S(1)}, bf16[4,3,1,128]{3,1,2,0:T(4,128)(2,1)S(1)}, u32[]{:S(2)}, u32[]{:S(2)}) collective-permute-start(bf16[4,3,1,128]{3,1,2,0:T(4,128)(2,1)S(1)} %copy.94), channel_id=1, source_target_pairs={{0,1},{1,2},{2,3},{3,4},{4,5},{5,6},{6,7},{8,9},{9,10},{10,11},{11... | collective-permute-start | bytes 9224 | tf_op jit(solution)/shard_map/ppermute | solution.py:14
  45.5 4.9 %collective-permute-start.1 = (bf16[4,3,1,128]{3,1,2,0:T(4,128)(2,1)S(1)}, bf16[4,3,1,128]{3,1,2,0:T(4,128)(2,1)S(1)}, u32[]{:S(2)}, u32[]{:S(2)}) collective-permute-start(bf16[4,3,1,128]{3,1,2,0:T(4,128)(2,1)S(1)} %copy.95), channel_id=1, source_target_pairs={{1,0},{2,1},{3,2},{4,3},{5,4},{6,5},{7,6},{9,8},{10,9},{11,10},{12... | collective-permute-start | bytes 9224 | tf_op jit(solution)/shard_map/ppermute | solution.py:17
  50.5 3.7 %collective-permute-start.2 = (bf16[2,3,10,128]{3,1,2,0:T(4,128)(2,1)S(1)}, bf16[2,3,10,128]{3,1,2,0:T(4,128)(2,1)S(1)}, u32[]{:S(2)}, u32[]{:S(2)}) collective-permute-start(bf16[2,3,10,128]{3,1,2,0:T(4,128)(2,1)S(1)} %slice.235), channel_id=1, source_target_pairs={{0,8},{8,16},{16,24},{24,32},{32,40},{40,48},{48,56},{56,64},{64,7... | collective-permute-start | bytes 46088 | tf_op jit(solution)/shard_map/ppermute | solution.py:25
  56.9 0.9 copy-start.5
  57.8 1.1 copy-start.6
  59.5 30.4 %collective-permute-start.3 = (bf16[4,96,1,128]{3,1,2,0:T(8,128)(2,1)S(1)}, bf16[4,96,1,128]{3,1,2,0:T(8,128)(2,1)S(1)}, u32[]{:S(2)}, u32[]{:S(2)}) collective-permute-start(bf16[4,96,1,128]{3,1,2,0:T(8,128)(2,1)S(1)} %get-tuple-element.27), channel_id=1, source_target_pairs={{0,1},{1,2},{2,3},{3,4},{4,5},{5,6},{6,7},{8,9},{9,10},{10,11},{11... | collective-permute-start | bytes 294920 | tf_op jit(solution)/shard_map/ppermute | solution.py:14
  62.3 27.6 %collective-permute-start.4 = (bf16[4,96,1,128]{3,1,2,0:T(8,128)(2,1)S(1)}, bf16[4,96,1,128]{3,1,2,0:T(8,128)(2,1)S(1)}, u32[]{:S(2)}, u32[]{:S(2)}) collective-permute-start(bf16[4,96,1,128]{3,1,2,0:T(8,128)(2,1)S(1)} %get-tuple-element.28), channel_id=1, source_target_pairs={{1,0},{2,1},{3,2},{4,3},{5,4},{6,5},{7,6},{9,8},{10,9},{11,10},{12... | collective-permute-start | bytes 294920 | tf_op jit(solution)/shard_map/ppermute | solution.py:17
  90.9 14.4 %collective-permute-start.5 = (bf16[2,96,10,128]{3,1,2,0:T(8,128)(2,1)}, bf16[2,96,10,128]{3,1,2,0:T(8,128)(2,1)S(1)}, u32[]{:S(2)}, u32[]{:S(2)}) collective-permute-start(bf16[2,96,10,128]{3,1,2,0:T(8,128)(2,1)} %slice.240), channel_id=1, source_target_pairs={{0,8},{8,16},{16,24},{24,32},{32,40},{40,48},{48,56},{56,64},{64,7... | collective-permute-start | bytes 1474568 | tf_op jit(solution)/shard_map/ppermute | solution.py:25
  105.7 1.1 copy-start.2
  112.6 0.9 copy-start.4
  123.6 53.0 %all-to-all-start.1 = ((bf16[64,32,384]{2,1,0:T(8,128)(2,1)}), bf16[64,32,384]{2,1,0:T(8,128)(2,1)S(1)}, u32[]{:S(2)}, u32[]{:S(2)}) async-start(bf16[64,32,384]{2,1,0:T(8,128)(2,1)} %bitcast.69), calls=%async_computation.1 | async-start | bytes 3145728 | tf_op jit(solution)/shard_map/all_to_all | solution.py:132
where the time goes:
time: 183 us; the launch traced here: 181 us
  starting transfers between devices  50.1 us (27%)
  other arithmetic  47.8 us (26%)
  local copies, waits for them, and re-layouts  41.2 us (23%)
  waiting for transfers between devices  29.2 us (16%)
  matrix products  12.6 us (7%)
    sort x2, other arithmetic, route_plan(): arrivals = jnp.argsort(outside, stable=True)[:per_device]  28.5 us
    all_to_all x1, waiting for transfers between devices, body(): lax.all_to_all(parcel, 'wide', split_axis=0, concat_axis=0, tiled=True)  24.6 us
    all_to_all x1, starting transfers between devices, body(): lax.all_to_all(outgoing, 'wide', split_axis=0, concat_axis=0, tiled=True)  17.1 us
    all_to_all x1, starting transfers between devices, body(): lax.all_to_all(parcel, 'wide', split_axis=0, concat_axis=0, tiled=True)  13.2 us
    dot_general x18, matrix products, causal_conv(): jnp.einsum('ok,fkyx->foyx', weight[row_tap, col_tap], window, preferred_e...  12.6 us
    ppermute x2, starting transfers between devices, with_halo(): lax.ppermute(lax.slice_in_dim(block, block.shape[dim] - width, None, axis...  9.04 us
    gather x2, local copies, waits for them, and re-layouts, route_plan(): arrival_slots = places[arrivals] % per_device  6.79 us
    ppermute x2, starting transfers between devices, from_behind(): return lax.ppermute(array, axis, pairs)  6.71 us
  transfers between devices with their start and end apart: 8, of which 5 were waited for; matrix products, arithmetic and copies ran while one was open for 36% of the time, Pallas kernels for 0%

commit v1 on v0

v1 whole, which is shorter than its diff:
```python
import jax
import jax.numpy as jnp
import numpy as np
from jax import lax
from jax.experimental import pallas as pl
from jax.experimental.pallas import tpu as pltpu
from jax.sharding import PartitionSpec as P

EPSILON = 1e-06
MESH = pl.DeviceIdType.MESH
BF = jnp.bfloat16
F32 = jnp.float32
RING = 8
CH = 96
TOK = 1024
FRAME_ROWS = 72
LEAD = 4
NT = (((1,), (1,)), ((), ()))
NN = (((1,), (0,)), ((), ()))


def placement_tables():
    perm = np.zeros((256, 96), np.float32)
    for row in range(20):
        region, inner = (0, 6 + row) if row < 2 else ((1, row - 2) if row < 10 else ((2, row - 10) if row < 18 else (3, row - 18)))
        for parity in range(2):
            for ch in range(3):
                perm[parity * 128 + row * 6 + parity * 3 + ch, region * 24 + ch * 8 + inner] = 1
    pick = np.zeros((2, 64, 128), np.float32)
    for parity in range(2):
        for pair in range(64):
            pick[parity, pair, 2 * pair + parity] = 1
    return perm, pick


def weight_table():
    table = np.zeros((84, 16 * 384), np.float32)
    for ry in range(4):
        for rx in range(4):
            base = (ry * 4 + rx) * 384
            for ky in range(3):
                for kx in range(3):
                    for kt in range(3):
                        for ch in range(3):
                            row, col = ry + ky, rx + kx
                            lane = (col // 2) * 36 + row * 6 + (col % 2) * 3 + ch
                            table[(ky * 3 + kx) * 9 + kt * 3 + ch, base + kt * 128 + lane] = 1
            for part in range(3):
                table[81 + part, base + 2 * 128 + 108 + part] = 1
    return table


def gather_kernel(
    pix, perm, pick, out, edge, own, s0, r0, s1, r1, local_sem, s2, r2, s3, r3, s4, r4
):
    w = lax.axis_index("wide")
    n = lax.axis_index("narrow")
    z, y = w // RING, w % RING
    x, c = n // 2, n % 2
    sibling = (w, x * 2 + 1 - c)
    near = x + 2 * c - 1
    near_ok = jnp.logical_and(near >= 0, near <= 3)
    major = (z, y)
    minor = (y, z)

    def wide_of(piece, maj, mnr):
        return maj * RING + mnr if piece == 0 else mnr * RING + maj

    def along_minor(piece, d):
        return (wide_of(piece, major[piece], (minor[piece] + d) % RING), n)

    def along_major(piece, d):
        return (wide_of(piece, (major[piece] + d) % RING, minor[piece]), n)

    barrier = pltpu.get_barrier_semaphore()
    pl.semaphore_signal(barrier, inc=1, device_id=sibling, device_id_type=MESH)
    for piece in range(2):
        for d in range(1, RING):
            pl.semaphore_signal(barrier, inc=1, device_id=along_minor(piece, d), device_id_type=MESH)

    for side in (1, 3):
        for core in range(2):
            beside = ((x + side) % 4) * 2 + core
            pl.semaphore_signal(barrier, inc=1, device_id=(w, beside), device_id_type=MESH)
    pl.semaphore_wait(barrier, 19)

    def to_sibling():
        return pltpu.make_async_remote_copy(
            pix.at[pl.ds(2 * (1 - c), 2)], edge.at[0], s0.at[0], r0.at[0], sibling, MESH
        )

    def to_near(core):
        return pltpu.make_async_remote_copy(
            pix.at[pl.ds(2 * core, 2)],
            edge.at[2 - c],
            s0.at[1 + core],
            r0.at[2 - c],
            (w, jnp.clip(near, 0, 3) * 2 + core),
            MESH,
        )

    def arrival(region):
        return pltpu.make_async_remote_copy(
            pix.at[pl.ds(0, 2)], edge.at[region], s0.at[0], r0.at[region], sibling, MESH
        )

    to_sibling().start()

    @pl.when(near_ok)
    def _():
        to_near(0).start()
        to_near(1).start()

    @pl.when(x == 0)
    def _():
        edge[1] = jnp.zeros_like(edge[1])

    @pl.when(x == 3)
    def _():
        edge[2] = jnp.zeros_like(edge[2])

    arrival(0).wait_recv()

    @pl.when(x > 0)
    def _():
        arrival(1).wait_recv()

    @pl.when(x < 3)
    def _():
        arrival(2).wait_recv()

    for piece in range(2):
        mine = pix[2 * c + piece].astype(F32).reshape(24, 128)
        other = edge[0, piece].astype(F32).reshape(24, 128)
        low = edge[1, piece].astype(F32).reshape(24, 128)
        high = edge[2, piece].astype(F32).reshape(24, 128)
        first = jnp.where(c == 0, mine, other)
        second = jnp.where(c == 0, other, mine)
        stack = jnp.concatenate([low, first, second, high], axis=0).astype(BF)
        spread = lax.dot_general(perm[...], stack, NN, preferred_element_type=F32).astype(BF)
        rows = lax.dot_general(pick[0], spread[:128], NT, preferred_element_type=F32)
        rows += lax.dot_general(pick[1], spread[128:], NT, preferred_element_type=F32)
        own[piece] = rows.astype(BF)

    def local(piece):
        return pltpu.make_async_copy(
            own.at[piece], out.at[piece, c, major[piece], minor[piece]], local_sem.at[piece]
        )

    def first_hop(piece, d, slot):
        return pltpu.make_async_remote_copy(
            own.at[piece],
            out.at[piece, c, major[piece], slot],
            s1.at[piece, d],
            r1.at[piece, d],
            along_minor(piece, d),
            MESH,
        )

    order = (1, 7, 2, 6, 3, 5, 4)
    for d in order:
        for piece in range(2):
            first_hop(piece, d, minor[piece]).start()
    for piece in range(2):
        local(piece).start()

    def part(piece, chunk, h):
        return out.at[piece, c, chunk, pl.ds(4 * h, 4)]

    def hop(piece, way, k, h):
        step = 1 - 2 * way
        chunk = (major[piece] - step * (k - 1)) % RING
        ref = part(piece, chunk, h)
        return pltpu.make_async_remote_copy(
            ref, ref, s2.at[piece, way, k - 1, h], r2.at[piece, way, k - 1, h], along_major(piece, step), MESH
        )

    def landed(piece, way, k, h):
        step = 1 - 2 * way
        ref = part(piece, (major[piece] - step * k) % RING, h)
        return pltpu.make_async_remote_copy(
            ref, ref, s2.at[piece, way, k - 1, h], r2.at[piece, way, k - 1, h], along_major(piece, step), MESH
        )

    def share(piece, way, k, h, core):
        step = 1 - 2 * way
        ref = out.at[piece, core, (major[piece] - step * k) % RING, pl.ds(4 * h, 4)]
        return pltpu.make_async_remote_copy(
            ref, ref, s3.at[piece, way, k - 1, h], r3.at[piece, way, k - 1, h], sibling, MESH
        )

    def share_own(piece, core):
        ref = out.at[piece, core, major[piece]]
        return pltpu.make_async_remote_copy(ref, ref, s4.at[piece], r4.at[piece], sibling, MESH)

    for piece in range(2):
        local(piece).wait()
        for d in order:
            first_hop(piece, d, (minor[piece] - d) % RING).wait_recv()
        for i in range(2):
            for way in range(2):
                hop(piece, way, 1, i if way == 0 else 1 - i).start()
        share_own(piece, c).start()

    moves = []
    for k in range(1, 5):
        for i in range(2):
            for piece in range(2):
                for way in range(2):
                    h = i if way == 0 else 1 - i
                    if k < 4 or i == 0:
                        moves.append((piece, way, k, h, k < 3 or (k == 3 and i == 0)))
    for piece, way, k, h, onward in moves:
        landed(piece, way, k, h).wait_recv()
        if onward:
            hop(piece, way, k + 1, h).start()
        share(piece, way, k, h, c).start()

    to_sibling().wait_send()

    @pl.when(near_ok)
    def _():
        to_near(0).wait_send()
        to_near(1).wait_send()

    for piece in range(2):
        for d in order:
            first_hop(piece, d, minor[piece]).wait_send()
        share_own(piece, c).wait_send()
        share_own(piece, 1 - c).wait_recv()
    for piece, way, k, h, onward in moves:
        hop(piece, way, k, h).wait_send()
        share(piece, way, k, h, c).wait_send()
        share(piece, way, k, h, 1 - c).wait_recv()


def gather_tables(pixel_slabs):
    perm, pick = placement_tables()
    dma = pltpu.SemaphoreType.DMA
    vmem = pl.BlockSpec(memory_space=pltpu.VMEM)
    return pl.pallas_call(
        gather_kernel,
        out_shape=jax.ShapeDtypeStruct((2, 2, RING, RING, 64, 128), BF),
        in_specs=[vmem, vmem, vmem],
        out_specs=pl.BlockSpec(memory_space=pl.ANY),
        scratch_shapes=[
            pltpu.VMEM((3, 2, 3, 8, 128), BF),
            pltpu.VMEM((2, 64, 128), BF),
            dma((3,)),
            dma((3,)),
            dma((2, RING)),
            dma((2, RING)),
            dma((2,)),
            dma((2, 2, 4, 2)),
            dma((2, 2, 4, 2)),
            dma((2, 2, 4, 2)),
            dma((2, 2, 4, 2)),
            dma((2,)),
            dma((2,)),
        ],
        compiler_params=pltpu.CompilerParams(collective_id=0, has_side_effects=True),
        name="gather_tables",
    )(pixel_slabs, jnp.asarray(perm, BF), jnp.asarray(pick, BF))


def plan_kernel(tok, out):
    base = lax.axis_index("wide") * TOK
    sub = lax.broadcasted_iota(jnp.int32, (32, 256), 0)
    high_of = (sub % 8) * 4 + sub // 8
    lane = lax.broadcasted_iota(jnp.int32, (1, 256), 1)

    def step(t, total):
        row = tok[pl.ds(t, 1), :] - base
        hit = jnp.broadcast_to(row // 32, (32, 256)) == high_of
        one = jnp.broadcast_to(row % 32, (32, 256)) == sub
        times = jnp.where(hit, t.astype(F32), 0.0)
        inner = jnp.where(hit, jnp.broadcast_to(lane, (32, 256)).astype(F32), 0.0)
        left = jnp.concatenate([times, inner], axis=0).astype(BF)
        right = jnp.where(one, 1.0, 0.0).astype(BF)
        return total + lax.dot_general(left, right, NT, preferred_element_type=F32)

    total = lax.fori_loop(0, 256, step, jnp.zeros((64, 32), F32), unroll=8)
    entry = (total[:32] * 256.0 + total[32:]).astype(jnp.int32)
    out[...] = jnp.concatenate([entry[8 * m : 8 * m + 8] for m in range(4)], axis=1)


def invert_plan(tok_place):
    vmem = pl.BlockSpec(memory_space=pltpu.VMEM)
    return pl.pallas_call(
        plan_kernel,
        out_shape=jax.ShapeDtypeStruct((8, 128), jnp.int32),
        in_specs=[vmem],
        out_specs=vmem,
        name="invert_plan",
    )(tok_place.reshape(256, 256))


TILE = 256


def main_kernel(
    entry_s, slab_s, clip_s, entry_v, table, taps, spread, weight, gain, bias2, out, frames, patches, w1, w2, hid, act
):
    n = lax.axis_index("narrow")
    x, c = n // 2, n % 2

    for pos in range(16):
        w1[pos * CH : (pos + 1) * CH, :] = lax.dot_general(
            taps[...], spread[:, pos * 384 : (pos + 1) * 384], NN, preferred_element_type=F32
        ).astype(BF)
    zero = jnp.zeros((CH, CH), F32)
    for kt in range(3):
        for dy in range(2):
            for dx in range(2):
                blocks = []
                for ry in range(4):
                    for rx in range(4):
                        ky, kx = ry - dy, rx - dx
                        inside = 0 <= ky < 3 and 0 <= kx < 3
                        blocks.append(
                            weight[ky, kx, :, kt * CH : (kt + 1) * CH].astype(F32) if inside else zero
                        )
                row = (dy * 2 + dx) * CH
                w2[kt, row : row + CH, :] = jnp.concatenate(blocks, axis=1).astype(BF)

    frames[0 : LEAD * FRAME_ROWS, :] = jnp.zeros((LEAD * FRAME_ROWS, 128), F32)
    frames[(LEAD + 256) * FRAME_ROWS : (LEAD + 256) * FRAME_ROWS + 8, :] = jnp.zeros((8, 128), F32)

    def fill(i, carry):
        piece, core, maj, mnr = i // 128, (i // 64) % 2, (i // 8) % 8, i % 8
        wide = jnp.where(piece == 0, maj * RING + mnr, mnr * RING + maj)
        frame = slab_s[wide * 4 + core * 2 + piece]
        at = pl.multiple_of((frame + LEAD) * FRAME_ROWS, 8)
        frames[pl.ds(at, 8), :] = jnp.zeros((8, 128), F32)
        frames[pl.ds(at + 8, 64), :] = table[i].astype(F32)
        return carry

    lax.fori_loop(0, 256, fill, 0, unroll=4)

    starts = []
    running = jnp.int32(0)
    for i in range(6):
        starts.append(running)
        running = running + clip_s[i]

    lane = lax.broadcasted_iota(jnp.int32, (5, 128), 1)
    when = lax.broadcasted_iota(jnp.int32, (5, 128), 0)

    def pull(s, carry):
        e = entry_s[s]
        t, j, col = e // 256, (e // 64) % 4, e % 64
        latest = jnp.int32(0)
        for i in range(1, 6):
            latest = jnp.where(starts[i] <= t, starts[i], latest)
        base = t * FRAME_ROWS + 7 + col
        turn = 128 - (4 * c + j) * 12
        left = frames[pl.ds(base, 5, stride=FRAME_ROWS), :]
        mid = frames[pl.ds(base + 1, 5, stride=FRAME_ROWS), :]
        right = frames[pl.ds(base + 2, 5, stride=FRAME_ROWS), :]
        left = pltpu.roll(left, turn % 128, 1)
        mid = pltpu.roll(mid, (turn + 36) % 128, 1)
        right = pltpu.roll(right, (turn + 72) % 128, 1)
        row = jnp.where(lane < 36, left, jnp.where(lane < 72, mid, jnp.where(lane < 108, right, 1.0)))
        row = jnp.where(when >= 4 - (t - latest), row, 0.0)
        patches[pl.ds(s, 5, stride=TOK), :] = row
        return carry

    lax.fori_loop(0, TOK, pull, 0, unroll=8)

    half_gain = gain[...] * 0.5

    def tile(g, carry):
        at = pl.multiple_of(g * TILE, TILE)
        e = entry_v[:, pl.ds(at, TILE)]
        t, j, col = e // 256, (e // 64) % 4, e % 64
        latest = jnp.zeros_like(t)
        for i in range(1, 6):
            latest = jnp.where(starts[i] <= t, starts[i], latest)
        age = t - latest
        row_ok = [
            jnp.logical_not(jnp.logical_and(j == 0, n == 0)),
            None,
            None,
            jnp.logical_not(jnp.logical_and(j == 3, n == 7)),
        ]
        col_ok = [col != 0, None, None, col != 63]
        total = jnp.zeros((4 * CH, TILE), F32) + bias2[...]
        for s in range(3):
            block = jnp.concatenate(
                [patches[pl.ds(pl.multiple_of((s + kt) * TOK + at, TILE), TILE), :].astype(BF) for kt in range(3)],
                axis=1,
            )
            hid[...] = lax.dot_general(w1[...], block, NT, preferred_element_type=F32)
            for ry in range(4):
                for rx in range(4):
                    pos = ry * 4 + rx
                    h = hid[pos * CH : (pos + 1) * CH, :]
                    scale = lax.rsqrt(jnp.sum(h * h, axis=0, keepdims=True) * (1.0 / CH) + EPSILON)
                    ok = age >= 2 - s
                    if row_ok[ry] is not None:
                        ok = jnp.logical_and(ok, row_ok[ry])
                    if col_ok[rx] is not None:
                        ok = jnp.logical_and(ok, col_ok[rx])
                    u = h * jnp.where(ok, scale, 0.0) * half_gain
                    act[pos * CH : (pos + 1) * CH, :] = (u + u * jnp.tanh(u)).astype(BF)
            total = total + lax.dot_general(w2[s], act[...], NN, preferred_element_type=F32)
            if s == 2:
                keep = [hid[(ry * 4 + rx) * CH : (ry * 4 + rx + 1) * CH, :] for ry in (1, 2) for rx in (1, 2)]
                total = total + jnp.concatenate(keep, axis=0)
        out[pl.ds(at, TILE), :] = jnp.transpose(total).astype(BF)
        return carry

    lax.fori_loop(0, TOK // TILE, tile, 0)


def encode(entry, slab_place, clip_lengths, table, taps, weight, gain, bias2):
    vmem = pl.BlockSpec(memory_space=pltpu.VMEM)
    smem = pl.BlockSpec(memory_space=pltpu.SMEM)
    return pl.pallas_call(
        main_kernel,
        out_shape=jax.ShapeDtypeStruct((TOK, 4 * CH), BF),
        in_specs=[smem, smem, smem] + [vmem] * 7,
        out_specs=vmem,
        scratch_shapes=[
            pltpu.VMEM(((LEAD + 256) * FRAME_ROWS + 8, 128), F32),
            pltpu.VMEM((5 * TOK, 128), F32),
            pltpu.VMEM((16 * CH, 384), BF),
            pltpu.VMEM((3, 4 * CH, 16 * CH), BF),
            pltpu.VMEM((16 * CH, TILE), F32),
            pltpu.VMEM((16 * CH, TILE), BF),
        ],
        compiler_params=pltpu.CompilerParams(vmem_limit_bytes=56 << 20),
        name="encode",
    )(
        entry.reshape(TOK),
        slab_place,
        clip_lengths,
        entry.reshape(1, TOK),
        table,
        taps,
        jnp.asarray(weight_table(), BF),
        weight,
        gain.reshape(CH, 1),
        bias2.reshape(4 * CH, 1),
    )


def split_bias(bias):
    first = lax.reduce_precision(bias, 8, 7)
    second = lax.reduce_precision(bias - first, 8, 7)
    third = bias - first - second
    return jnp.stack([first, second, third], axis=1).astype(BF)


def body(
    pixel_slabs,
    conv_in_weight,
    conv_in_bias,
    norm_gain,
    conv_weight,
    conv_bias,
    clip_lengths,
    slab_place,
    tok_place,
):
    table = gather_tables(pixel_slabs)
    entry = invert_plan(tok_place)
    taps = jnp.transpose(conv_in_weight, (2, 0, 1, 3)).reshape(CH, 81)
    taps = jnp.concatenate([taps, split_bias(conv_in_bias)], axis=1)
    return encode(
        entry,
        slab_place,
        clip_lengths,
        table.reshape(256, 64, 128),
        taps,
        conv_weight,
        norm_gain,
        jnp.tile(conv_bias, 4),
    )


def solution(mesh):
    placed = (P("wide", None, "narrow", None), P(), P(), P(), P(), P(), P(), P(), P())
    return jax.shard_map(
        body, mesh=mesh, in_specs=placed, out_specs=P(("wide", "narrow"), None), check_vma=False
    )
```

time: 183 us -> 116 us (0.63)
  Pallas kernels: 0 us -> 108 us
  starting transfers between devices: 50.1 us -> 0 us
  other arithmetic: 47.8 us -> 1.37 us
  local copies, waits for them, and re-layouts: 41.2 us -> 5.85 us
  waiting for transfers between devices: 29.2 us -> 0 us
  matrix products: 12.6 us -> 0 us
    pallas_call x0 -> x3, Pallas kernels: none -> 108 us  [the longest x1 53.1 us: encode(): pl.pallas_call(main_kernel, out_shape=jax.ShapeDtypeStruct((TOK, 4 * CH),...]
    sort x8 -> x0, other arithmetic: 43.9 us -> none  [the longest x2 28.5 us: route_plan(): arrivals = jnp.argsort(outside, stable=True)[:per_device]]
    all_to_all x2 -> x0, starting transfers between devices: 30.3 us -> none  [the longest x1 17.1 us: body(): lax.all_to_all(outgoing, 'wide', split_axis=0, concat_axis=0, tiled=True)]
    gather x10 -> x0, local copies, waits for them, and re-layouts: 28.1 us -> none  [the longest x2 6.79 us: route_plan(): arrival_slots = places[arrivals] % per_device]
    all_to_all x2 -> x0, waiting for transfers between devices: 24.9 us -> none  [the longest x1 24.6 us: body(): lax.all_to_all(parcel, 'wide', split_axis=0, concat_axis=0, tiled=True)]
    ppermute x6 -> x0, starting transfers between devices: 19.8 us -> none  [the longest x2 9.04 us: with_halo(): lax.ppermute(lax.slice_in_dim(block, block.shape[dim] - width, None, axis...]
    dot_general x18 -> x0, matrix products: 12.6 us -> none  [causal_conv(): jnp.einsum('ok,fkyx->foyx', weight[row_tap, col_tap], window, preferred_e...]
    scatter x2 -> x0, local copies, waits for them, and re-layouts: 8.31 us -> none  [the longest x1 6.35 us: body(): jnp.zeros((wide_count * tok_cap, tokens.shape[1]), tokens.dtype)]
  transfers between devices with their start and end apart: 8 -> 0, of which waited for: 5 -> 0; matrix products, arithmetic and copies ran while one was open for 36% -> 0% of each run, Pallas kernels for 0% -> 0%
where the time goes in v1:
time: 116 us; the launch traced here: 115 us
  Pallas kernels  108 us (93%)
  local copies, waits for them, and re-layouts  5.85 us (5%)
  other arithmetic  1.37 us (1%)
    pallas_call x1, Pallas kernels, encode(): pl.pallas_call(main_kernel, out_shape=jax.ShapeDtypeStruct((TOK, 4 * CH),...  53.1 us
    pallas_call x1, Pallas kernels, gather_tables(): pl.pallas_call(gather_kernel, out_shape=jax.ShapeDtypeStruct((2, 2, RING,...  46 us
    pallas_call x1, Pallas kernels, invert_plan(): pl.pallas_call(plan_kernel, out_shape=jax.ShapeDtypeStruct((8, 128), jnp....  8.9 us

profile of v1, /device:TPU:1, one launch (start us, length us, event | category | flops | bytes accessed | tf_op | source)
XLA Modules:
  0.0 115.2 jit_solution(17891350069335356959)
XLA Ops:
  0.0 0.7 fusion
  0.7 0.7 tile.2
  1.3 0.1 copy.20
  1.4 0.1 copy.22
  1.6 0.1 copy.21
  1.7 0.8 copy.18
  2.5 0.1 copy.19
  2.6 0.7 pad_maximum_fusion.taps
  3.3 1.4 %copy.23.gain = f32[96,1]{1,0:T(8,128)} copy(f32[96,1]{0,1:T(1,128)} %bitcast.17) | data formatting | bytes 768 | tf_op jit(solution)/shard_map/reshape | solution.py:443
  4.7 0.8 reshape_tile.4.bias2
  5.5 1.7 %reshape.19.tok = s32[256,256]{1,0:T(8,128)} reshape(s32[65536]{0:T(1024)} %param.20) | data formatting | bytes 524288 | tf_op jit(solution)/shard_map/reshape | solution.py:295
  7.2 8.9 %invert_plan.1 = s32[8,128]{1,0:T(8,128)} custom-call(s32[256,256]{1,0:T(8,128)} %reshape.19.tok), custom_call_target="tpu_custom_call" | custom-call | tf_op jit(solution)/shard_map/invert_plan/pallas_call | solution.py:289
  16.1 46.0 %gather_tables.1 = bf16[2,2,8,8,64,128]{5,4,3,2,1,0:T(8,128)(2,1)} custom-call(bf16[4,3,8,128]{3,2,1,0:T(8,128)(2,1)} %pix.1, bf16[256,96]{1,0:T(8,128)(2,1)} %constant.6.clone.perm, bf16[2,64,128]{2,1,0:T(8,128)(2,1)} %constant.7.clone.pick), custom_call_target="tpu_custom_call" | custom-call | tf_op jit(solution)/shard_map/gather_tables/pallas_call | solution.py:241
  62.1 53.1 %encode.1 = bf16[1024,384]{1,0:T(8,128)(2,1)} custom-call(s32[1024]{0:T(1024)} %bitcast.14, s32[256]{0:T(256)} %slab_s.1, s32[6]{0:T(128)} %clip_s.1, s32[1,1024]{1,0:T(1,128)} %bitcast.15, bf16[256,64,128]{2,1,0:T(8,128)(2,1)} %bitcast.13, bf16[96,84]{1,0:T(8,128)(2,1)} %pad_maximum_fusion.taps, bf16[84,6144]{1,0:T(8,128)(2,1)} %constant.8.clone.spread, ...), custom_call_target="tpu_custom_call" | custom-call | tf_op jit(solution)/shard_map/encode/pallas_call | solution.py:419
  (1 shorter events, 0.0 us)

commit v2 on v1

--- a/solution.py
+++ b/solution.py
@@ -34,19 +34,21 @@
 
 
 def weight_table():
-    table = np.zeros((84, 16 * 384), np.float32)
-    for ry in range(4):
-        for rx in range(4):
-            base = (ry * 4 + rx) * 384
-            for ky in range(3):
-                for kx in range(3):
-                    for kt in range(3):
-                        for ch in range(3):
-                            row, col = ry + ky, rx + kx
-                            lane = (col // 2) * 36 + row * 6 + (col % 2) * 3 + ch
-                            table[(ky * 3 + kx) * 9 + kt * 3 + ch, base + kt * 128 + lane] = 1
-            for part in range(3):
-                table[81 + part, base + 2 * 128 + 108 + part] = 1
+    table = np.zeros((2, 84, 16 * 384), np.float32)
+    for core in range(2):
+        for ry in range(4):
+            for rx in range(4):
+                base = (ry * 4 + rx) * 384
+                for ky in range(3):
+                    for kx in range(3):
+                        for kt in range(3):
+                            for ch in range(3):
+                                row, col = ry + ky, rx + kx
+                                lane = (col // 2) * 36 + row * 6 + (col % 2) * 3 + ch
+                                lane = (lane + 48 * core) % 128
+                                table[core, (ky * 3 + kx) * 9 + kt * 3 + ch, base + kt * 128 + lane] = 1
+                for part in range(3):
+                    table[core, 81 + part, base + 2 * 128 + (108 + part + 48 * core) % 128] = 1
     return table
 
 
@@ -263,51 +265,105 @@
     )(pixel_slabs, jnp.asarray(perm, BF), jnp.asarray(pick, BF))
 
 
-def plan_kernel(tok, out):
+def clip_age(starts, t):
+    latest = jnp.zeros_like(t)
+    for i in range(1, 6):
+        latest = jnp.where(starts[i] <= t, starts[i], latest)
+    return t - latest
+
+
+def clip_starts(clip_s):
+    starts = [jnp.int32(0)]
+    for i in range(5):
+        starts.append(starts[-1] + clip_s[i])
+    return starts
+
+
+def plan_kernel(clip_s, tok, words, entry):
     base = lax.axis_index("wide") * TOK
     sub = lax.broadcasted_iota(jnp.int32, (32, 256), 0)
     high_of = (sub % 8) * 4 + sub // 8
-    lane = lax.broadcasted_iota(jnp.int32, (1, 256), 1)
+    inside = lax.broadcasted_iota(jnp.int32, (32, 256), 1).astype(F32)
 
     def step(t, total):
-        row = tok[pl.ds(t, 1), :] - base
-        hit = jnp.broadcast_to(row // 32, (32, 256)) == high_of
-        one = jnp.broadcast_to(row % 32, (32, 256)) == sub
+        pair = [jnp.broadcast_to(tok[pl.ds(2 * t + i, 1), :] - base, (32, 128)) for i in range(2)]
+        row = jnp.concatenate(pair, axis=1)
+        hit = row >> 5 == high_of
         times = jnp.where(hit, t.astype(F32), 0.0)
-        inner = jnp.where(hit, jnp.broadcast_to(lane, (32, 256)).astype(F32), 0.0)
+        inner = jnp.where(hit, inside, 0.0)
         left = jnp.concatenate([times, inner], axis=0).astype(BF)
-        right = jnp.where(one, 1.0, 0.0).astype(BF)
+        right = jnp.where(row & 31 == sub, 1.0, 0.0).astype(BF)
         return total + lax.dot_general(left, right, NT, preferred_element_type=F32)
 
     total = lax.fori_loop(0, 256, step, jnp.zeros((64, 32), F32), unroll=8)
-    entry = (total[:32] * 256.0 + total[32:]).astype(jnp.int32)
-    out[...] = jnp.concatenate([entry[8 * m : 8 * m + 8] for m in range(4)], axis=1)
-
-
-def invert_plan(tok_place):
+    found = (total[:32] * 256.0 + total[32:]).astype(jnp.int32)
+    e = jnp.concatenate([found[8 * m : 8 * m + 8] for m in range(4)], axis=1)
+    entry[...] = e
+    t, j, col = e >> 8, (e >> 6) & 3, e & 63
+    words[0:8, :] = t * FRAME_ROWS + 7 + col
+    words[8:16, :] = j
+    words[16:24, :] = 4 - clip_age(clip_starts(clip_s), t)
+
+
+def invert_plan(clip_lengths, tok_place):
     vmem = pl.BlockSpec(memory_space=pltpu.VMEM)
+    smem = pl.BlockSpec(memory_space=pltpu.SMEM)
     return pl.pallas_call(
         plan_kernel,
-        out_shape=jax.ShapeDtypeStruct((8, 128), jnp.int32),
-        in_specs=[vmem],
-        out_specs=vmem,
+        out_shape=(jax.ShapeDtypeStruct((24, 128), jnp.int32), jax.ShapeDtypeStruct((8, 128), jnp.int32)),
+        in_specs=[smem, vmem],
+        out_specs=(vmem, vmem),
         name="invert_plan",
-    )(tok_place.reshape(256, 256))
+    )(clip_lengths, tok_place.reshape(512, 128))
 
 
 TILE = 256
+BATCH = 8
+
+
+def column(row):
+    n = row.shape[1]
+    same = lax.broadcasted_iota(jnp.int32, (n, n), 0) == lax.broadcasted_iota(jnp.int32, (n, n), 1)
+    return jnp.sum(jnp.where(same, jnp.broadcast_to(row, (n, n)), 0.0), axis=1, keepdims=True)
 
 
 def main_kernel(
-    entry_s, slab_s, clip_s, entry_v, table, taps, spread, weight, gain, bias2, out, frames, patches, w1, w2, hid, act
+    words,
+    slab_s,
+    clip_s,
+    entry,
+    table,
+    spread_all,
+    in_weight,
+    in_bias,
+    gain,
+    weight,
+    bias,
+    out,
+    held,
+    spread,
+    frames,
+    patches,
+    shifts,
+    w1,
+    w2,
+    hid,
+    act,
+    load_sem,
+    spread_sem,
 ):
     n = lax.axis_index("narrow")
-    x, c = n // 2, n % 2
-
-    for pos in range(16):
-        w1[pos * CH : (pos + 1) * CH, :] = lax.dot_general(
-            taps[...], spread[:, pos * 384 : (pos + 1) * 384], NN, preferred_element_type=F32
-        ).astype(BF)
+    c = n % 2
+
+    def load(k):
+        return pltpu.make_async_copy(table.at[pl.ds(32 * k, 32)], held.at[pl.ds(32 * k, 32)], load_sem.at[k])
+
+    fetch = pltpu.make_async_copy(spread_all.at[c], spread, spread_sem)
+    for k in range(8):
+        load(k).start()
+        if k == 0:
+            fetch.start()
+
     zero = jnp.zeros((CH, CH), F32)
     for kt in range(3):
         for dy in range(2):
@@ -316,67 +372,79 @@
                 for ry in range(4):
                     for rx in range(4):
                         ky, kx = ry - dy, rx - dx
-                        inside = 0 <= ky < 3 and 0 <= kx < 3
+                        within = 0 <= ky < 3 and 0 <= kx < 3
                         blocks.append(
-                            weight[ky, kx, :, kt * CH : (kt + 1) * CH].astype(F32) if inside else zero
+                            weight[ky, kx, :, kt * CH : (kt + 1) * CH].astype(F32) if within else zero
                         )
                 row = (dy * 2 + dx) * CH
                 w2[kt, row : row + CH, :] = jnp.concatenate(blocks, axis=1).astype(BF)
 
+    half_gain = column(gain[...]) * 0.5
+    out_bias = column(bias[...])
+    first = column(in_bias[...])
+    split = []
+    for _ in range(3):
+        part = first.astype(BF).astype(F32)
+        split.append(part)
+        first = first - part
+    taps = [in_weight[ky, kx].astype(F32) for ky in range(3) for kx in range(3)]
+    taps = jnp.concatenate(taps + split, axis=1).astype(BF)
+    lane = lax.broadcasted_iota(jnp.int32, (8, 128), 1)
+    for j in range(4):
+        shifts[8 * j : 8 * j + 8, :] = (lane + 256 - (48 * c + 12 * j)) & 127
+    fetch.wait()
+    for pos in range(16):
+        w1[pos * CH : (pos + 1) * CH, :] = lax.dot_general(
+            taps, spread[:, pos * 384 : (pos + 1) * 384], NN, preferred_element_type=F32
+        ).astype(BF)
+
     frames[0 : LEAD * FRAME_ROWS, :] = jnp.zeros((LEAD * FRAME_ROWS, 128), F32)
     frames[(LEAD + 256) * FRAME_ROWS : (LEAD + 256) * FRAME_ROWS + 8, :] = jnp.zeros((8, 128), F32)
-
-    def fill(i, carry):
-        piece, core, maj, mnr = i // 128, (i // 64) % 2, (i // 8) % 8, i % 8
-        wide = jnp.where(piece == 0, maj * RING + mnr, mnr * RING + maj)
-        frame = slab_s[wide * 4 + core * 2 + piece]
-        at = pl.multiple_of((frame + LEAD) * FRAME_ROWS, 8)
-        frames[pl.ds(at, 8), :] = jnp.zeros((8, 128), F32)
-        frames[pl.ds(at + 8, 64), :] = table[i].astype(F32)
+    for k in range(8):
+        piece, core = k // 4, (k // 2) % 2
+        load(k).wait()
+
+        def fill(m, carry):
+            maj = (k % 2) * 4 + m
+            at = []
+            for mnr in range(RING):
+                wide = maj * RING + mnr if piece == 0 else mnr * RING + maj
+                frame = slab_s[wide * 4 + core * 2 + piece]
+                at.append(pl.multiple_of((frame + LEAD) * FRAME_ROWS, 8))
+            for mnr in range(RING):
+                frames[pl.ds(at[mnr], 8), :] = jnp.zeros((8, 128), F32)
+                frames[pl.ds(at[mnr] + 8, 64), :] = held[32 * k + m * RING + mnr].astype(F32)
+            return carry
+
+        lax.fori_loop(0, 4, fill, 0)
+
+    late = lax.broadcasted_iota(jnp.int32, (5, 128), 0)
+
+    def pick_up(s):
+        base, j, least = words[s], words[TOK + s], words[2 * TOK + s]
+        rel = shifts[pl.ds(pl.multiple_of(j * 8, 8), 5), :]
+        left = frames[pl.ds(base, 5, stride=FRAME_ROWS), :]
+        mid = pltpu.roll(frames[pl.ds(base + 1, 5, stride=FRAME_ROWS), :], 36, 1)
+        right = pltpu.roll(frames[pl.ds(base + 2, 5, stride=FRAME_ROWS), :], 72, 1)
+        row = jnp.where(rel < 36, left, jnp.where(rel < 72, mid, jnp.where(rel < 108, right, 1.0)))
+        row = jnp.where(late >= least, row, 0.0)
+        return pltpu.roll(row, 128 - 12 * j, 1)
+
+    def pull(q, carry):
+        rows = [pick_up(q * BATCH + i) for i in range(BATCH)]
+        for i in range(BATCH):
+            patches[pl.ds(q * BATCH + i, 5, stride=TOK), :] = rows[i]
         return carry
 
-    lax.fori_loop(0, 256, fill, 0, unroll=4)
-
-    starts = []
-    running = jnp.int32(0)
-    for i in range(6):
-        starts.append(running)
-        running = running + clip_s[i]
-
-    lane = lax.broadcasted_iota(jnp.int32, (5, 128), 1)
-    when = lax.broadcasted_iota(jnp.int32, (5, 128), 0)
-
-    def pull(s, carry):
-        e = entry_s[s]
-        t, j, col = e // 256, (e // 64) % 4, e % 64
-        latest = jnp.int32(0)
-        for i in range(1, 6):
-            latest = jnp.where(starts[i] <= t, starts[i], latest)
-        base = t * FRAME_ROWS + 7 + col
-        turn = 128 - (4 * c + j) * 12
-        left = frames[pl.ds(base, 5, stride=FRAME_ROWS), :]
-        mid = frames[pl.ds(base + 1, 5, stride=FRAME_ROWS), :]
-        right = frames[pl.ds(base + 2, 5, stride=FRAME_ROWS), :]
-        left = pltpu.roll(left, turn % 128, 1)
-        mid = pltpu.roll(mid, (turn + 36) % 128, 1)
-        right = pltpu.roll(right, (turn + 72) % 128, 1)
-        row = jnp.where(lane < 36, left, jnp.where(lane < 72, mid, jnp.where(lane < 108, right, 1.0)))
-        row = jnp.where(when >= 4 - (t - latest), row, 0.0)
-        patches[pl.ds(s, 5, stride=TOK), :] = row
-        return carry
-
-    lax.fori_loop(0, TOK, pull, 0, unroll=8)
-
-    half_gain = gain[...] * 0.5
+    lax.fori_loop(0, TOK // BATCH, pull, 0)
+
+    starts = clip_starts(clip_s)
 
     def tile(g, carry):
         at = pl.multiple_of(g * TILE, TILE)
-        e = entry_v[:, pl.ds(at, TILE)]
-        t, j, col = e // 256, (e // 64) % 4, e % 64
-        latest = jnp.zeros_like(t)
-        for i in range(1, 6):
-            latest = jnp.where(starts[i] <= t, starts[i], latest)
-        age = t - latest
+        e = jnp.concatenate([entry[pl.ds(g * (TILE // 128) + i, 1), :] for i in range(TILE // 128)], axis=1)
+        t, j, col = e >> 8, (e >> 6) & 3, e & 63
+        age = clip_age(starts, t)
         row_ok = [
             jnp.logical_not(jnp.logical_and(j == 0, n == 0)),
             None,
@@ -384,7 +452,7 @@
             jnp.logical_not(jnp.logical_and(j == 3, n == 7)),
         ]
         col_ok = [col != 0, None, None, col != 63]
-        total = jnp.zeros((4 * CH, TILE), F32) + bias2[...]
+        total = jnp.concatenate([jnp.broadcast_to(out_bias, (CH, TILE))] * 4, axis=0)
         for s in range(3):
             block = jnp.concatenate(
                 [patches[pl.ds(pl.multiple_of((s + kt) * TOK + at, TILE), TILE), :].astype(BF) for kt in range(3)],
@@ -413,43 +481,43 @@
     lax.fori_loop(0, TOK // TILE, tile, 0)
 
 
-def encode(entry, slab_place, clip_lengths, table, taps, weight, gain, bias2):
+def encode(words, entry, slab_place, clip_lengths, table, in_weight, in_bias, gain, weight, bias):
     vmem = pl.BlockSpec(memory_space=pltpu.VMEM)
     smem = pl.BlockSpec(memory_space=pltpu.SMEM)
+    anywhere = pl.BlockSpec(memory_space=pl.ANY)
     return pl.pallas_call(
         main_kernel,
         out_shape=jax.ShapeDtypeStruct((TOK, 4 * CH), BF),
-        in_specs=[smem, smem, smem] + [vmem] * 7,
+        in_specs=[smem, smem, smem, vmem, anywhere, anywhere] + [vmem] * 5,
         out_specs=vmem,
         scratch_shapes=[
+            pltpu.VMEM((256, 64, 128), BF),
+            pltpu.VMEM((84, 16 * 384), BF),
             pltpu.VMEM(((LEAD + 256) * FRAME_ROWS + 8, 128), F32),
             pltpu.VMEM((5 * TOK, 128), F32),
+            pltpu.VMEM((32, 128), jnp.int32),
             pltpu.VMEM((16 * CH, 384), BF),
             pltpu.VMEM((3, 4 * CH, 16 * CH), BF),
             pltpu.VMEM((16 * CH, TILE), F32),
             pltpu.VMEM((16 * CH, TILE), BF),
+            pltpu.SemaphoreType.DMA((8,)),
+            pltpu.SemaphoreType.DMA,
         ],
         compiler_params=pltpu.CompilerParams(vmem_limit_bytes=56 << 20),
         name="encode",
     )(
-        entry.reshape(TOK),
+        words.reshape(3 * TOK),
         slab_place,
         clip_lengths,
-        entry.reshape(1, TOK),
+        entry,
         table,
-        taps,
         jnp.asarray(weight_table(), BF),
+        in_weight,
+        in_bias.reshape(1, CH),
+        gain.reshape(1, CH),
         weight,
-        gain.reshape(CH, 1),
-        bias2.reshape(4 * CH, 1),
+        bias.reshape(1, CH),
     )
-
-
-def split_bias(bias):
-    first = lax.reduce_precision(bias, 8, 7)
-    second = lax.reduce_precision(bias - first, 8, 7)
-    third = bias - first - second
-    return jnp.stack([first, second, third], axis=1).astype(BF)
 
 
 def body(
@@ -464,18 +532,18 @@
     tok_place,
 ):
     table = gather_tables(pixel_slabs)
-    entry = invert_plan(tok_place)
-    taps = jnp.transpose(conv_in_weight, (2, 0, 1, 3)).reshape(CH, 81)
-    taps = jnp.concatenate([taps, split_bias(conv_in_bias)], axis=1)
+    words, entry = invert_plan(clip_lengths, tok_place)
     return encode(
+        words,
         entry,
         slab_place,
         clip_lengths,
         table.reshape(256, 64, 128),
-        taps,
+        conv_in_weight,
+        conv_in_bias,
+        norm_gain,
         conv_weight,
-        norm_gain,
-        jnp.tile(conv_bias, 4),
+        conv_bias,
     )
 
 

time: 116 us -> 97 us (0.84)
  Pallas kernels: 108 us -> 95.2 us
  local copies, waits for them, and re-layouts: 5.85 us -> 1.59 us
  other arithmetic: 1.37 us -> 0 us
    pallas_call x1, Pallas kernels: 53.1 us -> 40.6 us  [encode(): pl.pallas_call(main_kernel, out_shape=jax.ShapeDtypeStruct((TOK, 4 * CH),...]
    reshape x4 -> x0, local copies, waits for them, and re-layouts: 3.23 us -> none  [the longest x1 1.72 us: invert_plan(): tok_place.reshape(256, 256)]
    another operation x5 -> x0, local copies, waits for them, and re-layouts: 1.87 us -> none  [the longest x1 0.84 us: encode(): bias2.reshape(4 * CH, 1)]
    unnamed x0 -> x1, local copies, waits for them, and re-layouts: none -> 1.59 us
where the time goes in v2:
time: 97 us; the launch traced here: 96.7 us
  Pallas kernels  95.2 us (98%)
  local copies, waits for them, and re-layouts  1.59 us (2%)
    pallas_call x1, Pallas kernels, gather_tables(): pl.pallas_call(gather_kernel, out_shape=jax.ShapeDtypeStruct((2, 2, RING,...  46 us
    pallas_call x1, Pallas kernels, encode(): pl.pallas_call(main_kernel, out_shape=jax.ShapeDtypeStruct((TOK, 4 * CH),...  40.6 us
    pallas_call x1, Pallas kernels, invert_plan(): pl.pallas_call(plan_kernel, out_shape=(jax.ShapeDtypeStruct((24, 128), jn...  8.51 us

profile of v2, /device:TPU:1, one launch (start us, length us, event | category | flops | bytes accessed | tf_op | source)
XLA Modules:
  0.0 96.7 jit_solution(13321334787866026470)
XLA Ops:
  0.0 8.5 %invert_plan.1 = (s32[24,128]{1,0:T(8,128)}, s32[8,128]{1,0:T(8,128)}) custom-call(s32[6]{0:T(128)} %clip_s.3, s32[512,128]{1,0:T(8,128)} %bitcast.7), custom_call_target="tpu_custom_call" | custom-call | tf_op jit(solution)/shard_map/invert_plan/pallas_call | solution.py:311
  8.5 1.6 %copy.13.in_weight = bf16[3,3,96,9]{3,2,1,0:T(8,128)(2,1)} copy(bf16[3,3,96,9]{2,1,3,0:T(4,128)(2,1)} %param.13) | data formatting | bytes 31104 | tf_op args[1]
  10.1 46.0 %gather_tables.1 = bf16[2,2,8,8,64,128]{5,4,3,2,1,0:T(8,128)(2,1)} custom-call(bf16[4,3,8,128]{3,2,1,0:T(8,128)(2,1)} %pix.1, bf16[256,96]{1,0:T(8,128)(2,1)} %constant.6.clone.perm, bf16[2,64,128]{2,1,0:T(8,128)(2,1)} %constant.7.clone.pick), custom_call_target="tpu_custom_call" | custom-call | tf_op jit(solution)/shard_map/gather_tables/pallas_call | solution.py:243
  56.1 40.6 %encode.1 = bf16[1024,384]{1,0:T(8,128)(2,1)} custom-call(s32[3072]{0:T(1024)} %bitcast.8, s32[256]{0:T(256)} %slab_s.1, s32[6]{0:T(128)} %clip_s.3, s32[8,128]{1,0:T(8,128)} %get-tuple-element.8.entry, bf16[256,64,128]{2,1,0:T(8,128)(2,1)} %bitcast.6, bf16[2,84,6144]{2,1,0:T(8,128)(2,1)} %constant.8.clone.spread_all, bf16[3,3,96,9]{3,2,1,0:T(8,128)(2,1)} %copy.13.in_weight, ...), custom_call_target="tpu_custom_call" | custom-call | tf_op jit(solution)/shard_map/encode/pallas_call | solution.py:488

commit v3 on v2

--- a/solution.py
+++ b/solution.py
@@ -46,14 +46,65 @@
                                 row, col = ry + ky, rx + kx
                                 lane = (col // 2) * 36 + row * 6 + (col % 2) * 3 + ch
                                 lane = (lane + 48 * core) % 128
-                                table[core, (ky * 3 + kx) * 9 + kt * 3 + ch, base + kt * 128 + lane] = 1
+                                table[core, (ky * 9 + kt * 3 + ch) * 3 + kx, base + kt * 128 + lane] = 1
                 for part in range(3):
                     table[core, 81 + part, base + 2 * 128 + (108 + part + 48 * core) % 128] = 1
     return table
 
 
+def clip_age(starts, t):
+    latest = jnp.zeros_like(t)
+    for i in range(1, 6):
+        latest = jnp.where(starts[i] <= t, starts[i], latest)
+    return t - latest
+
+
+def clip_starts(clip_s):
+    starts = [jnp.int32(0)]
+    for i in range(5):
+        starts.append(starts[-1] + clip_s[i])
+    return starts
+
+
+PLAN = 1024
+
+
+def plan_steps(tok, total, base, first, last):
+    sub = lax.broadcasted_iota(jnp.int32, (32, PLAN), 0)
+    high_of = (sub % 8) * 4 + sub // 8
+    lane = lax.broadcasted_iota(jnp.int32, (32, PLAN), 1)
+    inside = (lane % 256).astype(F32)
+    frame = (lane // 256).astype(F32)
+
+    def step(q, carry):
+        rows = tok[pl.ds(pl.multiple_of(q * 8, 8), 8), :] - base
+        row = jnp.concatenate([jnp.broadcast_to(rows[i : i + 1], (32, 128)) for i in range(8)], axis=1)
+        hit = row >> 5 == high_of
+        times = jnp.where(hit, frame + (q * (PLAN // 256)).astype(F32), 0.0)
+        inner = jnp.where(hit, inside, 0.0)
+        left = jnp.concatenate([times, inner], axis=0).astype(BF)
+        right = jnp.where(row & 31 == sub, 1.0, 0.0).astype(BF)
+        total[...] += lax.dot_general(left, right, NT, preferred_element_type=F32)
+        return carry
+
+    lax.fori_loop(first, last, step, 0)
+
+
+def plan_words(total, starts, words, entry):
+    found = (total[:32, :] * 256.0 + total[32:, :]).astype(jnp.int32)
+    e = jnp.concatenate([found[8 * m : 8 * m + 8] for m in range(4)], axis=1)
+    entry[...] = e
+    t, j, col = e >> 8, (e >> 6) & 3, e & 63
+    words[0:8, :] = t * FRAME_ROWS + 7 + col
+    words[8:16, :] = j
+    words[16:24, :] = 4 - clip_age(starts, t)
+
+
+SUBS = 2
+
+
 def gather_kernel(
-    pix, perm, pick, out, edge, own, s0, r0, s1, r1, local_sem, s2, r2, s3, r3, s4, r4
+    clip_s, pix, tok, perm, pick, out, words, entry, own, edge, total, s0, r0, s1, r1, keep, s2, r2, s3, r3, s4, r4
 ):
     w = lax.axis_index("wide")
     n = lax.axis_index("narrow")
@@ -145,9 +196,7 @@
         own[piece] = rows.astype(BF)
 
     def local(piece):
-        return pltpu.make_async_copy(
-            own.at[piece], out.at[piece, c, major[piece], minor[piece]], local_sem.at[piece]
-        )
+        return pltpu.make_async_copy(own.at[piece], out.at[piece, c, major[piece], minor[piece]], keep.at[piece])
 
     def first_hop(piece, d, slot):
         return pltpu.make_async_remote_copy(
@@ -159,64 +208,66 @@
             MESH,
         )
 
-    order = (1, 7, 2, 6, 3, 5, 4)
-    for d in order:
-        for piece in range(2):
+    order = (4, 3, 5, 2, 6, 1, 7)
+    for piece in range(2):
+        for d in order:
             first_hop(piece, d, minor[piece]).start()
     for piece in range(2):
         local(piece).start()
 
-    def part(piece, chunk, h):
-        return out.at[piece, c, chunk, pl.ds(4 * h, 4)]
-
-    def hop(piece, way, k, h):
+    total[...] = jnp.zeros_like(total)
+    plan_steps(tok, total, w * TOK, 0, PLAN_A)
+
+    part = RING // SUBS
+
+    def hop(piece, way, k, h, arrived):
         step = 1 - 2 * way
-        chunk = (major[piece] - step * (k - 1)) % RING
-        ref = part(piece, chunk, h)
+        chunk = (major[piece] - step * (k if arrived else k - 1)) % RING
+        ref = out.at[piece, c, chunk, pl.ds(part * h, part)]
         return pltpu.make_async_remote_copy(
             ref, ref, s2.at[piece, way, k - 1, h], r2.at[piece, way, k - 1, h], along_major(piece, step), MESH
         )
 
-    def landed(piece, way, k, h):
-        step = 1 - 2 * way
-        ref = part(piece, (major[piece] - step * k) % RING, h)
+    def share(piece, way, k, h, core):
+        chunk = (major[piece] - (1 - 2 * way) * k) % RING
+        where = (piece, core, chunk, pl.ds(part * h, part))
         return pltpu.make_async_remote_copy(
-            ref, ref, s2.at[piece, way, k - 1, h], r2.at[piece, way, k - 1, h], along_major(piece, step), MESH
+            out.at[where], out.at[where], s3.at[piece, way, k - 1, h], r3.at[piece, way, k - 1, h], sibling, MESH
         )
 
-    def share(piece, way, k, h, core):
-        step = 1 - 2 * way
-        ref = out.at[piece, core, (major[piece] - step * k) % RING, pl.ds(4 * h, 4)]
-        return pltpu.make_async_remote_copy(
-            ref, ref, s3.at[piece, way, k - 1, h], r3.at[piece, way, k - 1, h], sibling, MESH
-        )
-
     def share_own(piece, core):
-        ref = out.at[piece, core, major[piece]]
-        return pltpu.make_async_remote_copy(ref, ref, s4.at[piece], r4.at[piece], sibling, MESH)
+        where = (piece, core, major[piece])
+        return pltpu.make_async_remote_copy(out.at[where], out.at[where], s4.at[piece], r4.at[piece], sibling, MESH)
+
+    def turned(way, i):
+        return i if way == 0 else SUBS - 1 - i
 
     for piece in range(2):
         local(piece).wait()
-        for d in order:
+        for d in reversed(order):
             first_hop(piece, d, (minor[piece] - d) % RING).wait_recv()
-        for i in range(2):
+        for i in range(SUBS):
             for way in range(2):
-                hop(piece, way, 1, i if way == 0 else 1 - i).start()
+                hop(piece, way, 1, turned(way, i), False).start()
+    for piece in range(2):
         share_own(piece, c).start()
+
+    plan_steps(tok, total, w * TOK, PLAN_A, TOK * 64 // PLAN)
 
     moves = []
     for k in range(1, 5):
-        for i in range(2):
+        for i in range(SUBS):
             for piece in range(2):
                 for way in range(2):
-                    h = i if way == 0 else 1 - i
-                    if k < 4 or i == 0:
-                        moves.append((piece, way, k, h, k < 3 or (k == 3 and i == 0)))
+                    if k < 4 or i < SUBS // 2:
+                        moves.append((piece, way, k, turned(way, i), k < 3 or (k == 3 and i < SUBS // 2)))
     for piece, way, k, h, onward in moves:
-        landed(piece, way, k, h).wait_recv()
+        hop(piece, way, k, h, True).wait_recv()
         if onward:
-            hop(piece, way, k + 1, h).start()
+            hop(piece, way, k + 1, h, False).start()
         share(piece, way, k, h, c).start()
+
+    plan_words(total, clip_starts(clip_s), words, entry)
 
     to_sibling().wait_send()
 
@@ -231,94 +282,59 @@
         share_own(piece, c).wait_send()
         share_own(piece, 1 - c).wait_recv()
     for piece, way, k, h, onward in moves:
-        hop(piece, way, k, h).wait_send()
+        hop(piece, way, k, h, False).wait_send()
         share(piece, way, k, h, c).wait_send()
         share(piece, way, k, h, 1 - c).wait_recv()
 
 
-def gather_tables(pixel_slabs):
+PLAN_A = 40
+
+
+def gather_tables(pixel_slabs, clip_lengths, tok_place):
     perm, pick = placement_tables()
     dma = pltpu.SemaphoreType.DMA
     vmem = pl.BlockSpec(memory_space=pltpu.VMEM)
+    shape = (2, 2, RING, RING, 64, 128)
     return pl.pallas_call(
         gather_kernel,
-        out_shape=jax.ShapeDtypeStruct((2, 2, RING, RING, 64, 128), BF),
-        in_specs=[vmem, vmem, vmem],
-        out_specs=pl.BlockSpec(memory_space=pl.ANY),
+        out_shape=(
+            jax.ShapeDtypeStruct(shape, BF),
+            jax.ShapeDtypeStruct((24, 128), jnp.int32),
+            jax.ShapeDtypeStruct((8, 128), jnp.int32),
+        ),
+        in_specs=[pl.BlockSpec(memory_space=pltpu.SMEM), vmem, vmem, vmem, vmem],
+        out_specs=(pl.BlockSpec(memory_space=pl.ANY), vmem, vmem),
         scratch_shapes=[
+            pltpu.VMEM((2, 64, 128), BF),
             pltpu.VMEM((3, 2, 3, 8, 128), BF),
-            pltpu.VMEM((2, 64, 128), BF),
+            pltpu.VMEM((64, 32), F32),
             dma((3,)),
             dma((3,)),
             dma((2, RING)),
             dma((2, RING)),
             dma((2,)),
-            dma((2, 2, 4, 2)),
-            dma((2, 2, 4, 2)),
-            dma((2, 2, 4, 2)),
-            dma((2, 2, 4, 2)),
+            dma((2, 2, 4, SUBS)),
+            dma((2, 2, 4, SUBS)),
+            dma((2, 2, 4, SUBS)),
+            dma((2, 2, 4, SUBS)),
             dma((2,)),
             dma((2,)),
         ],
-        compiler_params=pltpu.CompilerParams(collective_id=0, has_side_effects=True),
+        compiler_params=pltpu.CompilerParams(
+            collective_id=0, has_side_effects=True, vmem_limit_bytes=12 << 20
+        ),
         name="gather_tables",
-    )(pixel_slabs, jnp.asarray(perm, BF), jnp.asarray(pick, BF))
-
-
-def clip_age(starts, t):
-    latest = jnp.zeros_like(t)
-    for i in range(1, 6):
-        latest = jnp.where(starts[i] <= t, starts[i], latest)
-    return t - latest
-
-
-def clip_starts(clip_s):
-    starts = [jnp.int32(0)]
-    for i in range(5):
-        starts.append(starts[-1] + clip_s[i])
-    return starts
-
-
-def plan_kernel(clip_s, tok, words, entry):
-    base = lax.axis_index("wide") * TOK
-    sub = lax.broadcasted_iota(jnp.int32, (32, 256), 0)
-    high_of = (sub % 8) * 4 + sub // 8
-    inside = lax.broadcasted_iota(jnp.int32, (32, 256), 1).astype(F32)
-
-    def step(t, total):
-        pair = [jnp.broadcast_to(tok[pl.ds(2 * t + i, 1), :] - base, (32, 128)) for i in range(2)]
-        row = jnp.concatenate(pair, axis=1)
-        hit = row >> 5 == high_of
-        times = jnp.where(hit, t.astype(F32), 0.0)
-        inner = jnp.where(hit, inside, 0.0)
-        left = jnp.concatenate([times, inner], axis=0).astype(BF)
-        right = jnp.where(row & 31 == sub, 1.0, 0.0).astype(BF)
-        return total + lax.dot_general(left, right, NT, preferred_element_type=F32)
-
-    total = lax.fori_loop(0, 256, step, jnp.zeros((64, 32), F32), unroll=8)
-    found = (total[:32] * 256.0 + total[32:]).astype(jnp.int32)
-    e = jnp.concatenate([found[8 * m : 8 * m + 8] for m in range(4)], axis=1)
-    entry[...] = e
-    t, j, col = e >> 8, (e >> 6) & 3, e & 63
-    words[0:8, :] = t * FRAME_ROWS + 7 + col
-    words[8:16, :] = j
-    words[16:24, :] = 4 - clip_age(clip_starts(clip_s), t)
-
-
-def invert_plan(clip_lengths, tok_place):
-    vmem = pl.BlockSpec(memory_space=pltpu.VMEM)
-    smem = pl.BlockSpec(memory_space=pltpu.SMEM)
-    return pl.pallas_call(
-        plan_kernel,
-        out_shape=(jax.ShapeDtypeStruct((24, 128), jnp.int32), jax.ShapeDtypeStruct((8, 128), jnp.int32)),
-        in_specs=[smem, vmem],
-        out_specs=(vmem, vmem),
-        name="invert_plan",
-    )(clip_lengths, tok_place.reshape(512, 128))
-
-
-TILE = 256
-BATCH = 8
+    )(
+        clip_lengths,
+        pixel_slabs,
+        tok_place.reshape(512, 128),
+        jnp.asarray(perm, BF),
+        jnp.asarray(pick, BF),
+    )
+
+
+TILE = 1024
+BATCH = 32
 
 
 def column(row):
@@ -340,7 +356,6 @@
     weight,
     bias,
     out,
-    held,
     spread,
     frames,
     patches,
@@ -349,20 +364,13 @@
     w2,
     hid,
     act,
-    load_sem,
     spread_sem,
 ):
     n = lax.axis_index("narrow")
     c = n % 2
 
-    def load(k):
-        return pltpu.make_async_copy(table.at[pl.ds(32 * k, 32)], held.at[pl.ds(32 * k, 32)], load_sem.at[k])
-
     fetch = pltpu.make_async_copy(spread_all.at[c], spread, spread_sem)
-    for k in range(8):
-        load(k).start()
-        if k == 0:
-            fetch.start()
+    fetch.start()
 
     zero = jnp.zeros((CH, CH), F32)
     for kt in range(3):
@@ -381,14 +389,14 @@
 
     half_gain = column(gain[...]) * 0.5
     out_bias = column(bias[...])
-    first = column(in_bias[...])
+    rest = in_bias[...]
     split = []
     for _ in range(3):
-        part = first.astype(BF).astype(F32)
+        part = rest.astype(BF).astype(F32)
         split.append(part)
-        first = first - part
-    taps = [in_weight[ky, kx].astype(F32) for ky in range(3) for kx in range(3)]
-    taps = jnp.concatenate(taps + split, axis=1).astype(BF)
+        rest = rest - part
+    taps = [in_weight[ky, i].astype(F32) for ky in range(3) for i in range(9)]
+    taps = jnp.transpose(jnp.concatenate(taps + split, axis=0)).astype(BF)
     lane = lax.broadcasted_iota(jnp.int32, (8, 128), 1)
     for j in range(4):
         shifts[8 * j : 8 * j + 8, :] = (lane + 256 - (48 * c + 12 * j)) & 127
@@ -402,7 +410,6 @@
     frames[(LEAD + 256) * FRAME_ROWS : (LEAD + 256) * FRAME_ROWS + 8, :] = jnp.zeros((8, 128), F32)
     for k in range(8):
         piece, core = k // 4, (k // 2) % 2
-        load(k).wait()
 
         def fill(m, carry):
             maj = (k % 2) * 4 + m
@@ -413,7 +420,7 @@
                 at.append(pl.multiple_of((frame + LEAD) * FRAME_ROWS, 8))
             for mnr in range(RING):
                 frames[pl.ds(at[mnr], 8), :] = jnp.zeros((8, 128), F32)
-                frames[pl.ds(at[mnr] + 8, 64), :] = held[32 * k + m * RING + mnr].astype(F32)
+                frames[pl.ds(at[mnr] + 8, 64), :] = table[32 * k + m * RING + mnr].astype(F32)
             return carry
 
         lax.fori_loop(0, 4, fill, 0)
@@ -488,10 +495,9 @@
     return pl.pallas_call(
         main_kernel,
         out_shape=jax.ShapeDtypeStruct((TOK, 4 * CH), BF),
-        in_specs=[smem, smem, smem, vmem, anywhere, anywhere] + [vmem] * 5,
+        in_specs=[smem, smem, smem, vmem, vmem, anywhere] + [vmem] * 5,
         out_specs=vmem,
         scratch_shapes=[
-            pltpu.VMEM((256, 64, 128), BF),
             pltpu.VMEM((84, 16 * 384), BF),
             pltpu.VMEM(((LEAD + 256) * FRAME_ROWS + 8, 128), F32),
             pltpu.VMEM((5 * TOK, 128), F32),
@@ -500,10 +506,9 @@
             pltpu.VMEM((3, 4 * CH, 16 * CH), BF),
             pltpu.VMEM((16 * CH, TILE), F32),
             pltpu.VMEM((16 * CH, TILE), BF),
-            pltpu.SemaphoreType.DMA((8,)),
             pltpu.SemaphoreType.DMA,
         ],
-        compiler_params=pltpu.CompilerParams(vmem_limit_bytes=56 << 20),
+        compiler_params=pltpu.CompilerParams(vmem_limit_bytes=44 << 20),
         name="encode",
     )(
         words.reshape(3 * TOK),
@@ -531,15 +536,14 @@
     slab_place,
     tok_place,
 ):
-    table = gather_tables(pixel_slabs)
-    words, entry = invert_plan(clip_lengths, tok_place)
+    table, words, entry = gather_tables(pixel_slabs, clip_lengths, tok_place)
     return encode(
         words,
         entry,
         slab_place,
         clip_lengths,
         table.reshape(256, 64, 128),
-        conv_in_weight,
+        jnp.transpose(conv_in_weight, (0, 3, 1, 2)),
         conv_in_bias,
         norm_gain,
         conv_weight,

time: 97 us -> 77.7 us (0.80)
  Pallas kernels: 95.2 us -> 66.3 us
  local copies, waits for them, and re-layouts: 1.59 us -> 10.7 us
    pallas_call x1, Pallas kernels: 40.6 us -> 21.3 us  [encode(): pl.pallas_call(main_kernel, out_shape=jax.ShapeDtypeStruct((TOK, 4 * CH),...]
    pallas_call x2 -> x1, Pallas kernels: 54.5 us -> 44.9 us  [gather_tables(): pl.pallas_call(gather_kernel, out_shape=(jax.ShapeDtypeStruct(shape, BF),...]
    unnamed x1 -> x26, local copies, waits for them, and re-layouts: 1.59 us -> 10.7 us
where the time goes in v3:
time: 77.7 us; the launch traced here: 77.1 us
  Pallas kernels  66.3 us (85%)
  local copies, waits for them, and re-layouts  10.7 us (14%)
    pallas_call x1, Pallas kernels, gather_tables(): pl.pallas_call(gather_kernel, out_shape=(jax.ShapeDtypeStruct(shape, BF),...  44.9 us
    pallas_call x1, Pallas kernels, encode(): pl.pallas_call(main_kernel, out_shape=jax.ShapeDtypeStruct((TOK, 4 * CH),...  21.3 us
    unnamed x26, local copies, waits for them, and re-layouts  10.7 us

profile of v3, /device:TPU:1, one launch (start us, length us, event | category | flops | bytes accessed | tf_op | source)
XLA Modules:
  0.0 77.1 jit_solution(3271440877463776934)
XLA Ops:
  0.0 0.0 copy-start.2
  0.0 0.9 %copy-done.2 = s32[65536]{0:T(1024)S(1)} copy-done((s32[65536]{0:T(1024)S(1)}, s32[65536]{0:T(1024)}, u32[]{:S(2)}) %copy-start.2) | copy-done | bytes 262168
  1.0 0.0 copy-start.3
  1.0 0.8 %copy-done.3 = bf16[256,96]{1,0:T(8,128)(2,1)S(1)} copy-done((bf16[256,96]{1,0:T(8,128)(2,1)S(1)}, bf16[256,96]{1,0:T(8,128)(2,1)}, u32[]{:S(2)}) %copy-start.3) | copy-done | bytes 49176
  1.8 0.0 copy-start.4
  1.8 0.8 copy-done.4
  2.5 0.0 copy-start.6
  2.6 0.7 copy-done.6
  3.3 0.0 copy-start.7
  3.3 0.7 copy-done.7
  3.9 44.9 %gather_tables.1 = (bf16[2,2,8,8,64,128]{5,4,3,2,1,0:T(8,128)(2,1)S(1)}, s32[24,128]{1,0:T(8,128)S(1)}, s32[8,128]{1,0:T(8,128)S(1)}) custom-call(s32[6]{0:T(128)S(1)} %copy-done.7, bf16[4,3,8,128]{3,2,1,0:T(8,128)(2,1)S(1)} %copy-done.6, s32[512,128]{1,0:T(8,128)S(1)} %bitcast.8, bf16[256,96]{1,0:T(8,128)(2,1)S(1)} %copy-done.3, ...), custom_call_target="tpu_custom_call" | custom-call | tf_op jit(solution)/shard_map/gather_tables/pallas_call | solution.py:298
  48.9 0.0 copy-start
  48.9 1.6 %copy-done = bf16[2,84,6144]{2,1,0:T(8,128)(2,1)S(1)} copy-done((bf16[2,84,6144]{2,1,0:T(8,128)(2,1)S(1)}, bf16[2,84,6144]{2,1,0:T(8,128)(2,1)}, u32[]{:S(2)}) %copy-start) | copy-done | bytes 2064408
  50.5 0.0 copy-start.1
  50.5 1.1 %copy-done.1 = bf16[3,3,96,288]{3,2,1,0:T(8,128)(2,1)S(1)} copy-done((bf16[3,3,96,288]{3,2,1,0:T(8,128)(2,1)S(1)}, bf16[3,3,96,288]{3,2,1,0:T(8,128)(2,1)}, u32[]{:S(2)}) %copy-start.1) | copy-done | bytes 497688
  51.6 0.0 copy-start.5
  51.6 0.7 copy-done.5
  52.3 0.0 copy-start.8
  52.3 0.7 copy-done.8
  53.0 0.7 copy-done.9
  53.7 0.7 copy-done.10
  54.3 0.7 copy-done.11
  55.0 0.7 copy-done.12
  55.6 21.3 %encode.1 = bf16[1024,384]{1,0:T(8,128)(2,1)} custom-call(s32[3072]{0:T(1024)S(1)} %bitcast.10, s32[256]{0:T(256)S(1)} %copy-done.9, s32[6]{0:T(128)S(1)} %copy-done.8, s32[8,128]{1,0:T(8,128)S(1)} %get-tuple-element.9.entry, bf16[256,64,128]{2,1,0:T(8,128)(2,1)S(1)} %bitcast.7, bf16[2,84,6144]{2,1,0:T(8,128)(2,1)S(1)} %copy-done, ...), custom_call_target="tpu_custom_call" | custom-call | tf_op jit(solution)/shard_map/encode/pallas_call | solution.py:495
  (4 shorter events, 0.0 us)
Async XLA Ops:
  0.0 0.9 %copy-start.2 = (s32[65536]{0:T(1024)S(1)}, s32[65536]{0:T(1024)}, u32[]{:S(2)}) copy-start(s32[65536]{0:T(1024)} %param.20) | copy-start | bytes 786436
  1.0 0.8 %copy-start.3 = (bf16[256,96]{1,0:T(8,128)(2,1)S(1)}, bf16[256,96]{1,0:T(8,128)(2,1)}, u32[]{:S(2)}) copy-start(bf16[256,96]{1,0:T(8,128)(2,1)} %constant.6.clone.perm) | copy-start | bytes 147460
  1.8 0.8 copy-start.4
  2.5 0.7 copy-start.6
  3.3 0.7 copy-start.7
  48.9 1.6 %copy-start = (bf16[2,84,6144]{2,1,0:T(8,128)(2,1)S(1)}, bf16[2,84,6144]{2,1,0:T(8,128)(2,1)}, u32[]{:S(2)}) copy-start(bf16[2,84,6144]{2,1,0:T(8,128)(2,1)} %constant.8.clone.spread_all) | copy-start | bytes 6193156
  50.5 1.1 %copy-start.1 = (bf16[3,3,96,288]{3,2,1,0:T(8,128)(2,1)S(1)}, bf16[3,3,96,288]{3,2,1,0:T(8,128)(2,1)}, u32[]{:S(2)}) copy-start(bf16[3,3,96,288]{3,2,1,0:T(8,128)(2,1)} %weight.1) | copy-start | bytes 1492996
  51.6 0.7 copy-start.5
  52.3 0.7 copy-start.8
  53.0 0.7 copy-start.9
  53.7 0.7 copy-start.10
  54.3 0.7 copy-start.11
  55.0 0.7 copy-start.12

commit v4 on v3

--- a/solution.py
+++ b/solution.py
@@ -100,11 +100,84 @@
     words[16:24, :] = 4 - clip_age(starts, t)
 
 
+def lay_weights(in_weight, in_bias, weight, spread, w1, w2):
+    zero = jnp.zeros((CH, CH), F32)
+    for kt in range(3):
+        for dy in range(2):
+            for dx in range(2):
+                blocks = []
+                for ry in range(4):
+                    for rx in range(4):
+                        ky, kx = ry - dy, rx - dx
+                        within = 0 <= ky < 3 and 0 <= kx < 3
+                        blocks.append(
+                            weight[ky, kx, :, kt * CH : (kt + 1) * CH].astype(F32) if within else zero
+                        )
+                row = (dy * 2 + dx) * CH
+                w2[kt, row : row + CH, :] = jnp.concatenate(blocks, axis=1).astype(BF)
+    rest = in_bias[...]
+    split = []
+    for _ in range(3):
+        part = rest.astype(BF).astype(F32)
+        split.append(part)
+        rest = rest - part
+    taps = [in_weight[ky, i].astype(F32) for ky in range(3) for i in range(9)]
+    taps = jnp.transpose(jnp.concatenate(taps + split, axis=0)).astype(BF)
+    for pos in range(16):
+        w1[pos * CH : (pos + 1) * CH, :] = lax.dot_general(
+            taps, spread[:, pos * 384 : (pos + 1) * 384], NN, preferred_element_type=F32
+        ).astype(BF)
+
+
 SUBS = 2
 
 
 def gather_kernel(
-    clip_s, pix, tok, perm, pick, out, words, entry, own, edge, total, s0, r0, s1, r1, keep, s2, r2, s3, r3, s4, r4
+    clip_hbm,
+    slab_hbm,
+    pix,
+    tok_hbm,
+    perm_hbm,
+    pick_hbm,
+    spread_hbm,
+    in_weight_hbm,
+    in_bias_hbm,
+    gain_hbm,
+    weight_hbm,
+    bias_hbm,
+    out,
+    words,
+    entry,
+    scales,
+    w1,
+    w2,
+    clip_s,
+    slab,
+    mine_v,
+    tok,
+    perm,
+    pick,
+    spread,
+    in_weight,
+    in_bias,
+    gain,
+    weight,
+    bias,
+    load_sem,
+    own,
+    edge,
+    total,
+    s0,
+    r0,
+    s1,
+    r1,
+    keep,
+    s2,
+    r2,
+    s3,
+    r3,
+    s4,
+    r4,
 ):
     w = lax.axis_index("wide")
     n = lax.axis_index("narrow")
@@ -125,6 +198,24 @@
     def along_major(piece, d):
         return (wide_of(piece, (major[piece] + d) % RING, minor[piece]), n)
 
+    pairs = [
+        (pix.at[pl.ds(2 * c, 2)], mine_v),
+        (perm_hbm, perm),
+        (pick_hbm, pick),
+        (tok_hbm, tok),
+        (spread_hbm.at[c], spread),
+        (in_weight_hbm, in_weight),
+        (in_bias_hbm, in_bias),
+        (weight_hbm, weight),
+        (clip_hbm, clip_s),
+        (slab_hbm, slab),
+        (gain_hbm, gain),
+        (bias_hbm, bias),
+    ]
+    loads = [pltpu.make_async_copy(src, dst, load_sem.at[i]) for i, (src, dst) in enumerate(pairs)]
+    for copy in loads:
+        copy.start()
+
     barrier = pltpu.get_barrier_semaphore()
     pl.semaphore_signal(barrier, inc=1, device_id=sibling, device_id_type=MESH)
     for piece in range(2):
@@ -182,17 +273,19 @@
     def _():
         arrival(2).wait_recv()
 
+    for copy in loads[:3]:
+        copy.wait()
     for piece in range(2):
-        mine = pix[2 * c + piece].astype(F32).reshape(24, 128)
+        mine = mine_v[piece].astype(F32).reshape(24, 128)
         other = edge[0, piece].astype(F32).reshape(24, 128)
         low = edge[1, piece].astype(F32).reshape(24, 128)
         high = edge[2, piece].astype(F32).reshape(24, 128)
         first = jnp.where(c == 0, mine, other)
         second = jnp.where(c == 0, other, mine)
         stack = jnp.concatenate([low, first, second, high], axis=0).astype(BF)
-        spread = lax.dot_general(perm[...], stack, NN, preferred_element_type=F32).astype(BF)
-        rows = lax.dot_general(pick[0], spread[:128], NT, preferred_element_type=F32)
-        rows += lax.dot_general(pick[1], spread[128:], NT, preferred_element_type=F32)
+        laid = lax.dot_general(perm[...], stack, NN, preferred_element_type=F32).astype(BF)
+        rows = lax.dot_general(pick[0], laid[:128], NT, preferred_element_type=F32)
+        rows += lax.dot_general(pick[1], laid[128:], NT, preferred_element_type=F32)
         own[piece] = rows.astype(BF)
 
     def local(piece):
@@ -215,8 +308,15 @@
     for piece in range(2):
         local(piece).start()
 
+    for copy in loads[3:]:
+        copy.wait()
     total[...] = jnp.zeros_like(total)
-    plan_steps(tok, total, w * TOK, 0, PLAN_A)
+    plan_steps(tok, total, w * TOK, 0, TOK * 64 // PLAN)
+    plan_words(total, clip_starts(clip_s), words, entry)
+    words[24:26, :] = slab[...]
+    scales[0:1, 0:CH] = gain[...]
+    scales[1:2, 0:CH] = bias[...]
+    lay_weights(in_weight, in_bias, weight, spread, w1, w2)
 
     part = RING // SUBS
 
@@ -251,8 +351,6 @@
                 hop(piece, way, 1, turned(way, i), False).start()
     for piece in range(2):
         share_own(piece, c).start()
-
-    plan_steps(tok, total, w * TOK, PLAN_A, TOK * 64 // PLAN)
 
     moves = []
     for k in range(1, 5):
@@ -267,8 +365,6 @@
             hop(piece, way, k + 1, h, False).start()
         share(piece, way, k, h, c).start()
 
-    plan_words(total, clip_starts(clip_s), words, entry)
-
     to_sibling().wait_send()
 
     @pl.when(near_ok)
@@ -287,10 +383,7 @@
         share(piece, way, k, h, 1 - c).wait_recv()
 
 
-PLAN_A = 40
-
-
-def gather_tables(pixel_slabs, clip_lengths, tok_place):
+def gather_tables(clip_lengths, slab_place, pixel_slabs, tok_place, in_weight, in_bias, gain, weight, bias):
     perm, pick = placement_tables()
     dma = pltpu.SemaphoreType.DMA
     vmem = pl.BlockSpec(memory_space=pltpu.VMEM)
@@ -299,12 +392,28 @@
         gather_kernel,
         out_shape=(
             jax.ShapeDtypeStruct(shape, BF),
-            jax.ShapeDtypeStruct((24, 128), jnp.int32),
+            jax.ShapeDtypeStruct((32, 128), jnp.int32),
             jax.ShapeDtypeStruct((8, 128), jnp.int32),
+            jax.ShapeDtypeStruct((8, 128), F32),
+            jax.ShapeDtypeStruct((16 * CH, 384), BF),
+            jax.ShapeDtypeStruct((3, 4 * CH, 16 * CH), BF),
         ),
-        in_specs=[pl.BlockSpec(memory_space=pltpu.SMEM), vmem, vmem, vmem, vmem],
-        out_specs=(pl.BlockSpec(memory_space=pl.ANY), vmem, vmem),
+        in_specs=[pl.BlockSpec(memory_space=pltpu.HBM)] * 12,
+        out_specs=(pl.BlockSpec(memory_space=pl.ANY), vmem, vmem, vmem, vmem, vmem),
         scratch_shapes=[
+            pltpu.SMEM((6,), jnp.int32),
+            pltpu.VMEM((2, 128), jnp.int32),
+            pltpu.VMEM((2, 3, 8, 128), BF),
+            pltpu.VMEM((512, 128), jnp.int32),
+            pltpu.VMEM((256, 96), BF),
+            pltpu.VMEM((2, 64, 128), BF),
+            pltpu.VMEM((84, 16 * 384), BF),
+            pltpu.VMEM((3, 9, 3, CH), BF),
+            pltpu.VMEM((1, CH), F32),
+            pltpu.VMEM((1, CH), F32),
+            pltpu.VMEM((3, 3, CH, 3 * CH), BF),
+            pltpu.VMEM((1, CH), F32),
+            dma((12,)),
             pltpu.VMEM((2, 64, 128), BF),
             pltpu.VMEM((3, 2, 3, 8, 128), BF),
             pltpu.VMEM((64, 32), F32),
@@ -321,15 +430,24 @@
             dma((2,)),
         ],
         compiler_params=pltpu.CompilerParams(
-            collective_id=0, has_side_effects=True, vmem_limit_bytes=12 << 20
+            collective_id=0, has_side_effects=True, vmem_limit_bytes=16 << 20
         ),
         name="gather_tables",
     )(
+        *[pltpu.with_memory_space_constraint(v, pltpu.HBM) for v in (
         clip_lengths,
+        slab_place.reshape(2, 128),
         pixel_slabs,
         tok_place.reshape(512, 128),
         jnp.asarray(perm, BF),
         jnp.asarray(pick, BF),
+        jnp.asarray(weight_table(), BF),
+        jnp.transpose(in_weight, (0, 3, 1, 2)),
+        in_bias.reshape(1, CH),
+        gain.reshape(1, CH),
+        weight,
+        bias.reshape(1, CH),
+        )]
     )
 
 
@@ -343,68 +461,15 @@
     return jnp.sum(jnp.where(same, jnp.broadcast_to(row, (n, n)), 0.0), axis=1, keepdims=True)
 
 
-def main_kernel(
-    words,
-    slab_s,
-    clip_s,
-    entry,
-    table,
-    spread_all,
-    in_weight,
-    in_bias,
-    gain,
-    weight,
-    bias,
-    out,
-    spread,
-    frames,
-    patches,
-    shifts,
-    w1,
-    w2,
-    hid,
-    act,
-    spread_sem,
-):
+def main_kernel(words, entry, least, table, scales, w1, w2, out, frames, patches, shifts, hid, act):
     n = lax.axis_index("narrow")
     c = n % 2
 
-    fetch = pltpu.make_async_copy(spread_all.at[c], spread, spread_sem)
-    fetch.start()
-
-    zero = jnp.zeros((CH, CH), F32)
-    for kt in range(3):
-        for dy in range(2):
-            for dx in range(2):
-                blocks = []
-                for ry in range(4):
-                    for rx in range(4):
-                        ky, kx = ry - dy, rx - dx
-                        within = 0 <= ky < 3 and 0 <= kx < 3
-                        blocks.append(
-                            weight[ky, kx, :, kt * CH : (kt + 1) * CH].astype(F32) if within else zero
-                        )
-                row = (dy * 2 + dx) * CH
-                w2[kt, row : row + CH, :] = jnp.concatenate(blocks, axis=1).astype(BF)
-
-    half_gain = column(gain[...]) * 0.5
-    out_bias = column(bias[...])
-    rest = in_bias[...]
-    split = []
-    for _ in range(3):
-        part = rest.astype(BF).astype(F32)
-        split.append(part)
-        rest = rest - part
-    taps = [in_weight[ky, i].astype(F32) for ky in range(3) for i in range(9)]
-    taps = jnp.transpose(jnp.concatenate(taps + split, axis=0)).astype(BF)
+    half_gain = column(scales[0:1, 0:CH]) * 0.5
+    out_bias = column(scales[1:2, 0:CH])
     lane = lax.broadcasted_iota(jnp.int32, (8, 128), 1)
     for j in range(4):
         shifts[8 * j : 8 * j + 8, :] = (lane + 256 - (48 * c + 12 * j)) & 127
-    fetch.wait()
-    for pos in range(16):
-        w1[pos * CH : (pos + 1) * CH, :] = lax.dot_general(
-            taps, spread[:, pos * 384 : (pos + 1) * 384], NN, preferred_element_type=F32
-        ).astype(BF)
 
     frames[0 : LEAD * FRAME_ROWS, :] = jnp.zeros((LEAD * FRAME_ROWS, 128), F32)
     frames[(LEAD + 256) * FRAME_ROWS : (LEAD + 256) * FRAME_ROWS + 8, :] = jnp.zeros((8, 128), F32)
@@ -416,7 +481,7 @@
             at = []
             for mnr in range(RING):
                 wide = maj * RING + mnr if piece == 0 else mnr * RING + maj
-                frame = slab_s[wide * 4 + core * 2 + piece]
+                frame = words[3 * TOK + wide * 4 + core * 2 + piece]
                 at.append(pl.multiple_of((frame + LEAD) * FRAME_ROWS, 8))
             for mnr in range(RING):
                 frames[pl.ds(at[mnr], 8), :] = jnp.zeros((8, 128), F32)
@@ -428,13 +493,13 @@
     late = lax.broadcasted_iota(jnp.int32, (5, 128), 0)
 
     def pick_up(s):
-        base, j, least = words[s], words[TOK + s], words[2 * TOK + s]
+        base, j, oldest = words[s], words[TOK + s], words[2 * TOK + s]
         rel = shifts[pl.ds(pl.multiple_of(j * 8, 8), 5), :]
         left = frames[pl.ds(base, 5, stride=FRAME_ROWS), :]
         mid = pltpu.roll(frames[pl.ds(base + 1, 5, stride=FRAME_ROWS), :], 36, 1)
         right = pltpu.roll(frames[pl.ds(base + 2, 5, stride=FRAME_ROWS), :], 72, 1)
         row = jnp.where(rel < 36, left, jnp.where(rel < 72, mid, jnp.where(rel < 108, right, 1.0)))
-        row = jnp.where(late >= least, row, 0.0)
+        row = jnp.where(late >= oldest, row, 0.0)
         return pltpu.roll(row, 128 - 12 * j, 1)
 
     def pull(q, carry):
@@ -445,13 +510,13 @@
 
     lax.fori_loop(0, TOK // BATCH, pull, 0)
 
-    starts = clip_starts(clip_s)
-
     def tile(g, carry):
         at = pl.multiple_of(g * TILE, TILE)
-        e = jnp.concatenate([entry[pl.ds(g * (TILE // 128) + i, 1), :] for i in range(TILE // 128)], axis=1)
-        t, j, col = e >> 8, (e >> 6) & 3, e & 63
-        age = clip_age(starts, t)
+        e, old = [
+            jnp.concatenate([ref[pl.ds(g * (TILE // 128) + i, 1), :] for i in range(TILE // 128)], axis=1)
+            for ref in (entry, least.at[pl.ds(16, 8)])
+        ]
+        j, col, age = (e >> 6) & 3, e & 63, 4 - old
         row_ok = [
             jnp.logical_not(jnp.logical_and(j == 0, n == 0)),
             None,
@@ -488,41 +553,23 @@
     lax.fori_loop(0, TOK // TILE, tile, 0)
 
 
-def encode(words, entry, slab_place, clip_lengths, table, in_weight, in_bias, gain, weight, bias):
+def encode(words, entry, table, scales, w1, w2):
     vmem = pl.BlockSpec(memory_space=pltpu.VMEM)
-    smem = pl.BlockSpec(memory_space=pltpu.SMEM)
-    anywhere = pl.BlockSpec(memory_space=pl.ANY)
     return pl.pallas_call(
         main_kernel,
         out_shape=jax.ShapeDtypeStruct((TOK, 4 * CH), BF),
-        in_specs=[smem, smem, smem, vmem, vmem, anywhere] + [vmem] * 5,
+        in_specs=[pl.BlockSpec(memory_space=pltpu.SMEM)] + [vmem] * 6,
         out_specs=vmem,
         scratch_shapes=[
-            pltpu.VMEM((84, 16 * 384), BF),
             pltpu.VMEM(((LEAD + 256) * FRAME_ROWS + 8, 128), F32),
             pltpu.VMEM((5 * TOK, 128), F32),
             pltpu.VMEM((32, 128), jnp.int32),
-            pltpu.VMEM((16 * CH, 384), BF),
-            pltpu.VMEM((3, 4 * CH, 16 * CH), BF),
             pltpu.VMEM((16 * CH, TILE), F32),
             pltpu.VMEM((16 * CH, TILE), BF),
-            pltpu.SemaphoreType.DMA,
         ],
-        compiler_params=pltpu.CompilerParams(vmem_limit_bytes=44 << 20),
+        compiler_params=pltpu.CompilerParams(vmem_limit_bytes=42 << 20),
         name="encode",
-    )(
-        words.reshape(3 * TOK),
-        slab_place,
-        clip_lengths,
-        entry,
-        table,
-        jnp.asarray(weight_table(), BF),
-        in_weight,
-        in_bias.reshape(1, CH),
-        gain.reshape(1, CH),
-        weight,
-        bias.reshape(1, CH),
-    )
+    )(words.reshape(4 * TOK), entry, words, table.reshape(256, 64, 128), scales, w1, w2)
 
 
 def body(
@@ -536,19 +583,18 @@
     slab_place,
     tok_place,
 ):
-    table, words, entry = gather_tables(pixel_slabs, clip_lengths, tok_place)
-    return encode(
-        words,
-        entry,
+    table, words, entry, scales, w1, w2 = gather_tables(
+        clip_lengths,
         slab_place,
-        clip_lengths,
-        table.reshape(256, 64, 128),
-        jnp.transpose(conv_in_weight, (0, 3, 1, 2)),
+        pixel_slabs,
+        tok_place,
+        conv_in_weight,
         conv_in_bias,
         norm_gain,
         conv_weight,
         conv_bias,
     )
+    return encode(words, entry, table, scales, w1, w2)
 
 
 def solution(mesh):

time: 77.7 us -> 69.1 us (0.89)
  local copies, waits for them, and re-layouts: 10.7 us -> 0 us
  Pallas kernels: 66.3 us -> 68.9 us
    unnamed x26 -> x0, local copies, waits for them, and re-layouts: 10.7 us -> none
    pallas_call x1, Pallas kernels: 44.9 us -> 49.2 us  [gather_tables(): pl.pallas_call(gather_kernel, out_shape=(jax.ShapeDtypeStruct(shape, BF),...]
    pallas_call x1, Pallas kernels: 21.3 us -> 19.8 us  [encode(): pl.pallas_call(main_kernel, out_shape=jax.ShapeDtypeStruct((TOK, 4 * CH),...]
where the time goes in v4:
time: 69.1 us; the launch traced here: 69 us
  Pallas kernels  68.9 us (100%)
    pallas_call x1, Pallas kernels, gather_tables(): pl.pallas_call(gather_kernel, out_shape=(jax.ShapeDtypeStruct(shape, BF),...  49.2 us
    pallas_call x1, Pallas kernels, encode(): pl.pallas_call(main_kernel, out_shape=jax.ShapeDtypeStruct((TOK, 4 * CH),...  19.8 us

profile of v4, /device:TPU:1, one launch (start us, length us, event | category | flops | bytes accessed | tf_op | source)
XLA Modules:
  0.0 69.0 jit_solution(3652403194888555802)
XLA Ops:
  0.0 49.2 %gather_tables.1 = (bf16[2,2,8,8,64,128]{5,4,3,2,1,0:T(8,128)(2,1)S(1)}, s32[32,128]{1,0:T(8,128)S(1)}, s32[8,128]{1,0:T(8,128)S(1)}, f32[8,128]{1,0:T(8,128)S(1...) custom-call(s32[6]{0:T(128)} %clip_hbm.1, s32[2,128]{1,0:T(2,128)} %bitcast.12, ...), custom_call_target="tpu_custom_call" | custom-call | tf_op jit(solution)/shard_map/gather_tables/pallas_call | solution.py:391
  49.2 19.8 %encode.1 = bf16[1024,384]{1,0:T(8,128)(2,1)} custom-call(s32[4096]{0:T(1024)S(1)} %bitcast.9, s32[8,128]{1,0:T(8,128)S(1)} %get-tuple-element.12.entry, s32[32,128]{1,0:T(8,128)S(1)} %get-tuple-element.11.least, bf16[256,64,128]{2,1,0:T(8,128)(2,1)S(1)} %bitcast.8, f32[8,128]{1,0:T(8,128)S(1)} %get-tuple-element.14.scales, ...), custom_call_target="tpu_custom_call" | custom-call | tf_op jit(solution)/shard_map/encode/pallas_call | solution.py:558

commit v5 on v4

--- a/solution.py
+++ b/solution.py
@@ -1,3 +1,5 @@
+import functools
+
 import jax
 import jax.numpy as jnp
 import numpy as np
@@ -71,23 +73,30 @@
 
 def plan_steps(tok, total, base, first, last):
     sub = lax.broadcasted_iota(jnp.int32, (32, PLAN), 0)
-    high_of = (sub % 8) * 4 + sub // 8
+    high_of = ((sub % 8) * 4 + sub // 8).astype(F32).astype(BF)
+    low_of = sub.astype(F32).astype(BF)
     lane = lax.broadcasted_iota(jnp.int32, (32, PLAN), 1)
-    inside = (lane % 256).astype(F32)
+    inside = (lane % 256).astype(F32).astype(BF)
     frame = (lane // 256).astype(F32)
+    none = jnp.zeros((32, PLAN), BF)
+    ones = jnp.ones((32, PLAN), BF)
+
+    def spread_rows(rows):
+        wide = [jnp.broadcast_to(rows[i : i + 1], (32, 128)).astype(BF) for i in range(8)]
+        return jnp.concatenate(wide, axis=1)
 
     def step(q, carry):
         rows = tok[pl.ds(pl.multiple_of(q * 8, 8), 8), :] - base
-        row = jnp.concatenate([jnp.broadcast_to(rows[i : i + 1], (32, 128)) for i in range(8)], axis=1)
-        hit = row >> 5 == high_of
-        times = jnp.where(hit, frame + (q * (PLAN // 256)).astype(F32), 0.0)
-        inner = jnp.where(hit, inside, 0.0)
-        left = jnp.concatenate([times, inner], axis=0).astype(BF)
-        right = jnp.where(row & 31 == sub, 1.0, 0.0).astype(BF)
+        high = spread_rows(jnp.clip(rows >> 5, -1, 64).astype(F32))
+        low = spread_rows((rows & 31).astype(F32))
+        hit = high == high_of
+        times = jnp.where(hit, (frame + (q * (PLAN // 256)).astype(F32)).astype(BF), none)
+        left = jnp.concatenate([times, jnp.where(hit, inside, none)], axis=0)
+        right = jnp.where(low == low_of, ones, none)
         total[...] += lax.dot_general(left, right, NT, preferred_element_type=F32)
         return carry
 
-    lax.fori_loop(first, last, step, 0)
+    lax.fori_loop(first, last, step, 0, unroll=4)
 
 
 def plan_words(total, starts, words, entry):
@@ -100,36 +109,40 @@
     words[16:24, :] = 4 - clip_age(starts, t)
 
 
-def lay_weights(in_weight, in_bias, weight, spread, w1, w2):
+def lay_second(weight, w2, kt, dy, dx):
     zero = jnp.zeros((CH, CH), F32)
-    for kt in range(3):
-        for dy in range(2):
-            for dx in range(2):
-                blocks = []
-                for ry in range(4):
-                    for rx in range(4):
-                        ky, kx = ry - dy, rx - dx
-                        within = 0 <= ky < 3 and 0 <= kx < 3
-                        blocks.append(
-                            weight[ky, kx, :, kt * CH : (kt + 1) * CH].astype(F32) if within else zero
-                        )
-                row = (dy * 2 + dx) * CH
-                w2[kt, row : row + CH, :] = jnp.concatenate(blocks, axis=1).astype(BF)
+    blocks = []
+    for ry in range(4):
+        for rx in range(4):
+            ky, kx = ry - dy, rx - dx
+            within = 0 <= ky < 3 and 0 <= kx < 3
+            blocks.append(weight[ky, kx, :, kt * CH : (kt + 1) * CH].astype(F32) if within else zero)
+    row = (dy * 2 + dx) * CH
+    w2[kt, row : row + CH, :] = jnp.concatenate(blocks, axis=1).astype(BF)
+
+
+def gather_taps(in_weight, in_bias, taps):
     rest = in_bias[...]
     split = []
     for _ in range(3):
         part = rest.astype(BF).astype(F32)
         split.append(part)
         rest = rest - part
-    taps = [in_weight[ky, i].astype(F32) for ky in range(3) for i in range(9)]
-    taps = jnp.transpose(jnp.concatenate(taps + split, axis=0)).astype(BF)
-    for pos in range(16):
+    rows = [in_weight[ky, i].astype(F32) for ky in range(3) for i in range(9)]
+    taps[...] = jnp.transpose(jnp.concatenate(rows + split, axis=0)).astype(BF)
+
+
+def lay_first(taps, spread, w1, ry):
+    for pos in range(4 * ry, 4 * ry + 4):
         w1[pos * CH : (pos + 1) * CH, :] = lax.dot_general(
-            taps, spread[:, pos * 384 : (pos + 1) * 384], NN, preferred_element_type=F32
+            taps[...], spread[:, pos * 384 : (pos + 1) * 384], NN, preferred_element_type=F32
         ).astype(BF)
 
 
 SUBS = 2
+PLAN_A = 64
+LAG = 12
+PACE = 1
 
 
 def gather_kernel(
@@ -164,6 +177,7 @@
     weight,
     bias,
     load_sem,
+    taps,
     own,
     edge,
     total,
@@ -311,12 +325,25 @@
     for copy in loads[3:]:
         copy.wait()
     total[...] = jnp.zeros_like(total)
-    plan_steps(tok, total, w * TOK, 0, TOK * 64 // PLAN)
-    plan_words(total, clip_starts(clip_s), words, entry)
-    words[24:26, :] = slab[...]
-    scales[0:1, 0:CH] = gain[...]
-    scales[1:2, 0:CH] = bias[...]
-    lay_weights(in_weight, in_bias, weight, spread, w1, w2)
+    plan_steps(tok, total, w * TOK, 0, PLAN_A)
+
+    def last_words():
+        plan_words(total, clip_starts(clip_s), words, entry)
+        words[24:26, :] = slab[...]
+        scales[0:1, 0:CH] = gain[...]
+        scales[1:2, 0:CH] = bias[...]
+
+    work = [
+        functools.partial(plan_steps, tok, total, w * TOK, q, q + 8) for q in range(PLAN_A, TOK * 64 // PLAN, 8)
+    ]
+    work += [functools.partial(gather_taps, in_weight, in_bias, taps), last_words]
+    work += [functools.partial(lay_first, taps, spread, w1, ry) for ry in range(4)]
+    work += [
+        functools.partial(lay_second, weight, w2, kt, dy, dx)
+        for kt in range(3)
+        for dy in range(2)
+        for dx in range(2)
+    ]
 
     part = RING // SUBS
 
@@ -359,27 +386,36 @@
                 for way in range(2):
                     if k < 4 or i < SUBS // 2:
                         moves.append((piece, way, k, turned(way, i), k < 3 or (k == 3 and i < SUBS // 2)))
-    for piece, way, k, h, onward in moves:
+    to_sibling().wait_send()
+
+    @pl.when(near_ok)
+    def _():
+        to_near(0).wait_send()
+        to_near(1).wait_send()
+
+    for at, (piece, way, k, h, onward) in enumerate(moves):
         hop(piece, way, k, h, True).wait_recv()
         if onward:
             hop(piece, way, k + 1, h, False).start()
         share(piece, way, k, h, c).start()
-
-    to_sibling().wait_send()
-
-    @pl.when(near_ok)
-    def _():
-        to_near(0).wait_send()
-        to_near(1).wait_send()
+        if at < 14:
+            first_hop(at % 2, order[at // 2], minor[at % 2]).wait_send()
+        if at >= LAG:
+            hop(*moves[at - LAG][:4], False).wait_send()
+            share(*moves[at - LAG][:4], c).wait_send()
+        for _ in range(PACE):
+            if work:
+                work.pop(0)()
+    for task in work:
+        task()
 
     for piece in range(2):
-        for d in order:
-            first_hop(piece, d, minor[piece]).wait_send()
         share_own(piece, c).wait_send()
         share_own(piece, 1 - c).wait_recv()
-    for piece, way, k, h, onward in moves:
-        hop(piece, way, k, h, False).wait_send()
-        share(piece, way, k, h, c).wait_send()
+    for at, (piece, way, k, h, onward) in enumerate(moves):
+        if at >= len(moves) - LAG:
+            hop(piece, way, k, h, False).wait_send()
+            share(piece, way, k, h, c).wait_send()
         share(piece, way, k, h, 1 - c).wait_recv()
 
 
@@ -414,6 +450,7 @@
             pltpu.VMEM((3, 3, CH, 3 * CH), BF),
             pltpu.VMEM((1, CH), F32),
             dma((12,)),
+            pltpu.VMEM((CH, 84), BF),
             pltpu.VMEM((2, 64, 128), BF),
             pltpu.VMEM((3, 2, 3, 8, 128), BF),
             pltpu.VMEM((64, 32), F32),

time: 69.1 us -> 63.6 us (0.920)
  Pallas kernels: 68.9 us -> 63.4 us
    pallas_call x1, Pallas kernels: 49.2 us -> 43.5 us  [gather_tables(): pl.pallas_call(gather_kernel, out_shape=(jax.ShapeDtypeStruct(shape, BF),...]
where the time goes in v5:
time: 63.6 us; the launch traced here: 63.5 us
  Pallas kernels  63.4 us (100%)
    pallas_call x1, Pallas kernels, gather_tables(): pl.pallas_call(gather_kernel, out_shape=(jax.ShapeDtypeStruct(shape, BF),...  43.5 us
    pallas_call x1, Pallas kernels, encode(): pl.pallas_call(main_kernel, out_shape=jax.ShapeDtypeStruct((TOK, 4 * CH),...  20 us

profile of v5, /device:TPU:1, one launch (start us, length us, event | category | flops | bytes accessed | tf_op | source)
XLA Modules:
  0.0 63.5 jit_solution(9718751219206470286)
XLA Ops:
  0.0 43.5 %gather_tables.1 = (bf16[2,2,8,8,64,128]{5,4,3,2,1,0:T(8,128)(2,1)S(1)}, s32[32,128]{1,0:T(8,128)S(1)}, s32[8,128]{1,0:T(8,128)S(1)}, f32[8,128]{1,0:T(8,128)S(1...) custom-call(s32[6]{0:T(128)} %clip_hbm.1, s32[2,128]{1,0:T(2,128)} %bitcast.12, ...), custom_call_target="tpu_custom_call" | custom-call | tf_op jit(solution)/shard_map/gather_tables/pallas_call | solution.py:427
  43.5 20.0 %encode.1 = bf16[1024,384]{1,0:T(8,128)(2,1)} custom-call(s32[4096]{0:T(1024)S(1)} %bitcast.9, s32[8,128]{1,0:T(8,128)S(1)} %get-tuple-element.12.entry, s32[32,128]{1,0:T(8,128)S(1)} %get-tuple-element.11.least, bf16[256,64,128]{2,1,0:T(8,128)(2,1)S(1)} %bitcast.8, f32[8,128]{1,0:T(8,128)S(1)} %get-tuple-element.14.scales, ...), custom_call_target="tpu_custom_call" | custom-call | tf_op jit(solution)/shard_map/encode/pallas_call | solution.py:595

commit v6 on v5

--- a/solution.py
+++ b/solution.py
@@ -35,22 +35,24 @@
     return perm, pick
 
 
+def slot_of(ry, rx):
+    return (rx // 2) * 8 + ry * 2 + rx % 2
+
+
 def weight_table():
-    table = np.zeros((2, 84, 16 * 384), np.float32)
-    for core in range(2):
-        for ry in range(4):
-            for rx in range(4):
-                base = (ry * 4 + rx) * 384
-                for ky in range(3):
-                    for kx in range(3):
-                        for kt in range(3):
-                            for ch in range(3):
-                                row, col = ry + ky, rx + kx
-                                lane = (col // 2) * 36 + row * 6 + (col % 2) * 3 + ch
-                                lane = (lane + 48 * core) % 128
-                                table[core, (ky * 9 + kt * 3 + ch) * 3 + kx, base + kt * 128 + lane] = 1
-                for part in range(3):
-                    table[core, 81 + part, base + 2 * 128 + (108 + part + 48 * core) % 128] = 1
+    table = np.zeros((84, 16 * 256), np.float32)
+    for ry in range(4):
+        for rx in range(4):
+            base = slot_of(ry, rx) * 256
+            for ky in range(3):
+                for kx in range(3):
+                    for kt in range(3):
+                        for ch in range(3):
+                            row, col = ry + ky, rx + kx
+                            lane = (col // 2 - rx // 2) * 36 + row * 6 + (col % 2) * 3 + ch
+                            table[(ky * 9 + kt * 3 + ch) * 3 + kx, base + kt * 72 + lane] = 1
+            for part in range(3):
+                table[81 + part, base + 216 + part] = 1
     return table
 
 
@@ -135,7 +137,7 @@
 def lay_first(taps, spread, w1, ry):
     for pos in range(4 * ry, 4 * ry + 4):
         w1[pos * CH : (pos + 1) * CH, :] = lax.dot_general(
-            taps[...], spread[:, pos * 384 : (pos + 1) * 384], NN, preferred_element_type=F32
+            taps[...], spread[:, pos * 256 : (pos + 1) * 256], NN, preferred_element_type=F32
         ).astype(BF)
 
 
@@ -217,7 +219,7 @@
         (perm_hbm, perm),
         (pick_hbm, pick),
         (tok_hbm, tok),
-        (spread_hbm.at[c], spread),
+        (spread_hbm, spread),
         (in_weight_hbm, in_weight),
         (in_bias_hbm, in_bias),
         (weight_hbm, weight),
@@ -431,7 +433,7 @@
             jax.ShapeDtypeStruct((32, 128), jnp.int32),
             jax.ShapeDtypeStruct((8, 128), jnp.int32),
             jax.ShapeDtypeStruct((8, 128), F32),
-            jax.ShapeDtypeStruct((16 * CH, 384), BF),
+            jax.ShapeDtypeStruct((16 * CH, 256), BF),
             jax.ShapeDtypeStruct((3, 4 * CH, 16 * CH), BF),
         ),
         in_specs=[pl.BlockSpec(memory_space=pltpu.HBM)] * 12,
@@ -443,7 +445,7 @@
             pltpu.VMEM((512, 128), jnp.int32),
             pltpu.VMEM((256, 96), BF),
             pltpu.VMEM((2, 64, 128), BF),
-            pltpu.VMEM((84, 16 * 384), BF),
+            pltpu.VMEM((84, 16 * 256), BF),
             pltpu.VMEM((3, 9, 3, CH), BF),
             pltpu.VMEM((1, CH), F32),
             pltpu.VMEM((1, CH), F32),
@@ -537,7 +539,7 @@
         right = pltpu.roll(frames[pl.ds(base + 2, 5, stride=FRAME_ROWS), :], 72, 1)
         row = jnp.where(rel < 36, left, jnp.where(rel < 72, mid, jnp.where(rel < 108, right, 1.0)))
         row = jnp.where(late >= oldest, row, 0.0)
-        return pltpu.roll(row, 128 - 12 * j, 1)
+        return pltpu.roll(row, (256 - 48 * c - 12 * j) & 127, 1)
 
     def pull(q, carry):
         rows = [pick_up(q * BATCH + i) for i in range(BATCH)]
@@ -561,17 +563,25 @@
             jnp.logical_not(jnp.logical_and(j == 3, n == 7)),
         ]
         col_ok = [col != 0, None, None, col != 63]
+        spot = lax.broadcasted_iota(jnp.int32, (TILE, 128), 1)
         total = jnp.concatenate([jnp.broadcast_to(out_bias, (CH, TILE))] * 4, axis=0)
         for s in range(3):
-            block = jnp.concatenate(
-                [patches[pl.ds(pl.multiple_of((s + kt) * TOK + at, TILE), TILE), :].astype(BF) for kt in range(3)],
-                axis=1,
-            )
-            hid[...] = lax.dot_general(w1[...], block, NT, preferred_element_type=F32)
+            seen = [patches[pl.ds(pl.multiple_of((s + kt) * TOK + at, TILE), TILE), :] for kt in range(3)]
+            for half in range(2):
+                start = seen[0] if half == 0 else pltpu.roll(seen[0], 92, 1)
+                middle = pltpu.roll(seen[1], 72 - 36 * half, 1)
+                end = pltpu.roll(seen[2], 16 if half == 0 else 108, 1)
+                left = jnp.where(spot < 72, start, middle).astype(BF)
+                right = jnp.where(spot < 16, middle, jnp.where(spot < 88, end, 1.0)).astype(BF)
+                rows = slice(half * 8 * CH, (half + 1) * 8 * CH)
+                hid[rows, :] = lax.dot_general(
+                    w1[rows, :], jnp.concatenate([left, right], axis=1), NT, preferred_element_type=F32
+                )
             for ry in range(4):
                 for rx in range(4):
                     pos = ry * 4 + rx
-                    h = hid[pos * CH : (pos + 1) * CH, :]
+                    slot = slot_of(ry, rx) * CH
+                    h = hid[slot : slot + CH, :]
                     scale = lax.rsqrt(jnp.sum(h * h, axis=0, keepdims=True) * (1.0 / CH) + EPSILON)
                     ok = age >= 2 - s
                     if row_ok[ry] is not None:
@@ -582,7 +592,7 @@
                     act[pos * CH : (pos + 1) * CH, :] = (u + u * jnp.tanh(u)).astype(BF)
             total = total + lax.dot_general(w2[s], act[...], NN, preferred_element_type=F32)
             if s == 2:
-                keep = [hid[(ry * 4 + rx) * CH : (ry * 4 + rx + 1) * CH, :] for ry in (1, 2) for rx in (1, 2)]
+                keep = [hid[slot_of(ry, rx) * CH : slot_of(ry, rx) * CH + CH, :] for ry in (1, 2) for rx in (1, 2)]
                 total = total + jnp.concatenate(keep, axis=0)
         out[pl.ds(at, TILE), :] = jnp.transpose(total).astype(BF)
         return carry

time: 63.6 us -> 61.6 us (0.969)
  Pallas kernels: 63.4 us -> 61.5 us
    pallas_call x1, Pallas kernels: 20 us -> 18 us  [encode(): pl.pallas_call(main_kernel, out_shape=jax.ShapeDtypeStruct((TOK, 4 * CH),...]
where the time goes in v6:
time: 61.6 us; the launch traced here: 61.5 us
  Pallas kernels  61.5 us (100%)
    pallas_call x1, Pallas kernels, gather_tables(): pl.pallas_call(gather_kernel, out_shape=(jax.ShapeDtypeStruct(shape, BF),...  43.5 us
    pallas_call x1, Pallas kernels, encode(): pl.pallas_call(main_kernel, out_shape=jax.ShapeDtypeStruct((TOK, 4 * CH),...  18 us

profile of v6, /device:TPU:1, one launch (start us, length us, event | category | flops | bytes accessed | tf_op | source)
XLA Modules:
  0.0 61.5 jit_solution(11398865049174863264)
XLA Ops:
  0.0 43.5 %gather_tables.1 = (bf16[2,2,8,8,64,128]{5,4,3,2,1,0:T(8,128)(2,1)S(1)}, s32[32,128]{1,0:T(8,128)S(1)}, s32[8,128]{1,0:T(8,128)S(1)}, f32[8,128]{1,0:T(8,128)S(1...) custom-call(s32[6]{0:T(128)} %clip_hbm.1, s32[2,128]{1,0:T(2,128)} %bitcast.12, ...), custom_call_target="tpu_custom_call" | custom-call | tf_op jit(solution)/shard_map/gather_tables/pallas_call | solution.py:429
  43.5 18.0 %encode.1 = bf16[1024,384]{1,0:T(8,128)(2,1)} custom-call(s32[4096]{0:T(1024)S(1)} %bitcast.9, s32[8,128]{1,0:T(8,128)S(1)} %get-tuple-element.12.entry, s32[32,128]{1,0:T(8,128)S(1)} %get-tuple-element.11.least, bf16[256,64,128]{2,1,0:T(8,128)(2,1)S(1)} %bitcast.8, f32[8,128]{1,0:T(8,128)S(1)} %get-tuple-element.14.scales, ...), custom_call_target="tpu_custom_call" | custom-call | tf_op jit(solution)/shard_map/encode/pallas_call | solution.py:605

commit v7 on v6

--- a/solution.py
+++ b/solution.py
@@ -500,7 +500,11 @@
     return jnp.sum(jnp.where(same, jnp.broadcast_to(row, (n, n)), 0.0), axis=1, keepdims=True)
 
 
-def main_kernel(words, entry, least, table, scales, w1, w2, out, frames, patches, shifts, hid, act):
+def main_kernel(
+    words_any, entry, least, table, scales, w1, w2, out, frames, patches, shifts, hid, act, words, words_sem
+):
+    fetch = pltpu.make_async_copy(words_any, words, words_sem)
+    fetch.start()
     n = lax.axis_index("narrow")
     c = n % 2
 
@@ -512,6 +516,7 @@
 
     frames[0 : LEAD * FRAME_ROWS, :] = jnp.zeros((LEAD * FRAME_ROWS, 128), F32)
     frames[(LEAD + 256) * FRAME_ROWS : (LEAD + 256) * FRAME_ROWS + 8, :] = jnp.zeros((8, 128), F32)
+    fetch.wait()
     for k in range(8):
         piece, core = k // 4, (k // 2) % 2
 
@@ -605,7 +610,7 @@
     return pl.pallas_call(
         main_kernel,
         out_shape=jax.ShapeDtypeStruct((TOK, 4 * CH), BF),
-        in_specs=[pl.BlockSpec(memory_space=pltpu.SMEM)] + [vmem] * 6,
+        in_specs=[pl.BlockSpec(memory_space=pl.ANY)] + [vmem] * 6,
         out_specs=vmem,
         scratch_shapes=[
             pltpu.VMEM(((LEAD + 256) * FRAME_ROWS + 8, 128), F32),
@@ -613,6 +618,8 @@
             pltpu.VMEM((32, 128), jnp.int32),
             pltpu.VMEM((16 * CH, TILE), F32),
             pltpu.VMEM((16 * CH, TILE), BF),
+            pltpu.SMEM((4 * TOK,), jnp.int32),
+            pltpu.SemaphoreType.DMA,
         ],
         compiler_params=pltpu.CompilerParams(vmem_limit_bytes=42 << 20),
         name="encode",

time: 61.6 us -> 61.5 us (level)
  no operation moved by 1% of the time
where the time goes in v7:
time: 61.5 us; the launch traced here: 61.4 us
  Pallas kernels  61.4 us (100%)
    pallas_call x1, Pallas kernels, gather_tables(): pl.pallas_call(gather_kernel, out_shape=(jax.ShapeDtypeStruct(shape, BF),...  43.5 us
    pallas_call x1, Pallas kernels, encode(): pl.pallas_call(main_kernel, out_shape=jax.ShapeDtypeStruct((TOK, 4 * CH),...  17.9 us

profile of v7, /device:TPU:1, one launch (start us, length us, event | category | flops | bytes accessed | tf_op | source)
XLA Modules:
  0.0 61.4 jit_solution(15915876192225436992)
XLA Ops:
  0.0 43.5 %gather_tables.1 = (bf16[2,2,8,8,64,128]{5,4,3,2,1,0:T(8,128)(2,1)S(1)}, s32[32,128]{1,0:T(8,128)S(1)}, s32[8,128]{1,0:T(8,128)S(1)}, f32[8,128]{1,0:T(8,128)S(1...) custom-call(s32[6]{0:T(128)} %clip_hbm.1, s32[2,128]{1,0:T(2,128)} %bitcast.12, ...), custom_call_target="tpu_custom_call" | custom-call | tf_op jit(solution)/shard_map/gather_tables/pallas_call | solution.py:429
  43.5 17.9 %encode.1 = bf16[1024,384]{1,0:T(8,128)(2,1)} custom-call(s32[4096]{0:T(1024)S(1)} %bitcast.9, s32[8,128]{1,0:T(8,128)S(1)} %get-tuple-element.12.entry, s32[32,128]{1,0:T(8,128)S(1)} %get-tuple-element.11.least, bf16[256,64,128]{2,1,0:T(8,128)(2,1)S(1)} %bitcast.8, f32[8,128]{1,0:T(8,128)S(1)} %get-tuple-element.14.scales, ...), custom_call_target="tpu_custom_call" | custom-call | tf_op jit(solution)/shard_map/encode/pallas_call | solution.py:610
